TPU v7x, 128 devices: a whole 4x4x4 slice. The times are simulated.
128 devices in a mesh: grp: 2 (over core), gx: 32 (over z_hi, y, x), gy: 2 (over z_lo).
Axes of the slice: x: 4, y: 4, z: 4 (z_hi: 2, z_lo: 2; z = z_hi * 2 + z_lo), core: 2. Of those that a mesh axis runs over, the one named last changes fastest.
Arguments:
- les_velocity: float32 [1024, 32, 3, 512], P('gx', 'gy', None, 'grp'), may hold values from -6 to 6
- mean_mach: float32 [512, 32], P('gx', 'gy'), may hold values from 0.2 to 0.6
- transfer_tiles: bfloat16 [256, 2, 2, 64, 64], P('gx', 'gy'), may hold values from -0.75 to 0.75
- intersection_offset: int32 [256], P('gx'), may hold values from -1 to 1, as said below
- acoustic_state: float32 [512, 32, 4, 512], P('gx', 'gy', None, 'grp'), may hold values from -6 to 6
Outputs:
- acoustic_out: float32 [512, 32, 4, 512], P('gx', 'gy', None, 'grp')
Inputs may be any that keep to these rules, and one draw needn't show every extreme that they name: `intersection_offset`: each value is -1 or 1. The first block of every gx shard has -1 and the last has 1, except that the first two blocks of the grid have 1 and the last two have -1.
All inputs are finite; a program needn't handle non-finite values.
Results may differ from a plain program's by a relative error of at most 0.018.
Values sent between devices are 32-bit elements; how exact they have to be, the bound alone decides.
A program may use at most 128 MiB of HBM per device.

v0:
```python
import jax
import jax.numpy as jnp
from jax import lax
from jax.sharding import PartitionSpec as P

STEPS = 2


eddy_step = 0.1
viscosity = 0.5
wave_step = 0.2
filter_weight = 0.2
derivative_weights = (0.770882380518, -0.166705904415, 0.02084314277)
filter_taps = (0.28739284246, -0.226146951809, 0.10630357877, -0.023853048191)
unit_moves = ((1, 0, 0), (0, 1, 0), (0, 0, 1))


def padded_2(block, sides, width):
    for axis, dim in sides:
        count = lax.axis_size(axis)
        forward = [(i, i + 1) for i in range(count - 1)]
        backward = [(target, source) for source, target in forward]
        low = lax.ppermute(
            lax.slice_in_dim(block, block.shape[dim] - width, None, axis=dim), axis, forward
        )
        high = lax.ppermute(lax.slice_in_dim(block, 0, width, axis=dim), axis, backward)
        block = jnp.concatenate([low, block, high], axis=dim)
    return block


def shifted(array, axis, by):
    length = lax.axis_size(axis)
    pairs = [(i, i + by) for i in range(length) if 0 <= i + by < length]
    return lax.ppermute(array, axis, pairs)


def window(array, along_x, along_y, along_z, margin):
    return array[
        margin + along_x : array.shape[0] - margin + along_x,
        margin + along_y : array.shape[1] - margin + along_y,
        :,
        margin + along_z : array.shape[3] - margin + along_z,
    ]


def eddy_terms(velocity):
    padded = padded_2(velocity, (("grp", 3), ("gx", 0), ("gy", 1)), 1)
    center = window(padded, 0, 0, 0, 1)
    grads = []
    laplace = -6.0 * center
    for move in unit_moves:
        ahead = window(padded, move[0], move[1], move[2], 1)
        behind = window(padded, -move[0], -move[1], -move[2], 1)
        grads.append(0.5 * (ahead - behind))
        laplace = laplace + ahead + behind
    vort_x = grads[1][:, :, 2] - grads[2][:, :, 1]
    vort_y = grads[2][:, :, 0] - grads[0][:, :, 2]
    vort_z = grads[0][:, :, 1] - grads[1][:, :, 0]
    lamb = jnp.stack(
        [
            vort_y * center[:, :, 2] - vort_z * center[:, :, 1],
            vort_z * center[:, :, 0] - vort_x * center[:, :, 2],
            vort_x * center[:, :, 1] - vort_y * center[:, :, 0],
        ],
        axis=2,
    )
    return (lamb, laplace)


def derivative(padded, move):
    total = None
    for index in range(3):
        reach = index + 1
        ahead = window(padded, reach * move[0], reach * move[1], reach * move[2], 3)
        behind = window(padded, -reach * move[0], -reach * move[1], -reach * move[2], 3)
        term = derivative_weights[index] * (ahead - behind)
        total = term if total is None else total + term
    return total


def rate(padded, mach, source):
    grads = [derivative(padded, move) for move in unit_moves]
    convect = mach[:, :, None, None] * grads[0]
    pressure_rate = -(convect[:, :, 0] + grads[0][:, :, 1] + grads[1][:, :, 2] + grads[2][:, :, 3])
    x_rate = -(convect[:, :, 1] + grads[0][:, :, 0]) - source[:, :, 0]
    y_rate = -(convect[:, :, 2] + grads[1][:, :, 0]) - source[:, :, 1]
    z_rate = -(convect[:, :, 3] + grads[2][:, :, 0]) - source[:, :, 2]
    return jnp.stack([pressure_rate, x_rate, y_rate, z_rate], axis=2)


def smooth(padded):
    center = window(padded, 0, 0, 0, 3)
    total = 3.0 * filter_taps[0] * center
    for move in unit_moves:
        for index in range(1, 4):
            ahead = window(padded, index * move[0], index * move[1], index * move[2], 3)
            behind = window(padded, -index * move[0], -index * move[1], -index * move[2], 3)
            total = total + filter_taps[index] * (ahead + behind)
    return center - filter_weight * total


def shallow_rim(state):
    return padded_2(state, (("grp", 3), ("gx", 0), ("gy", 1)), 3)


def attach(own, from_lower, from_upper):
    own = own.at[0].add(from_lower)
    return own.at[-1].add(from_upper)


def body(les_velocity, mean_mach, transfer_tiles, intersection_offset, acoustic_state):
    cells_x, width_y, components, depth = les_velocity.shape
    wave_x = cells_x // 2
    tiles = transfer_tiles[:, 0].astype(jnp.float32)
    blocks = tiles.shape[0]
    plane = tiles.shape[2]
    bricks = blocks // 2
    slot = jnp.arange(blocks, dtype=jnp.int32) // 2 + 1 + intersection_offset
    onehot = (slot[:, None] == jnp.arange(bricks + 2, dtype=jnp.int32)[None, :]).astype(jnp.float32)
    velocity = les_velocity
    sources = []
    for step in range(STEPS):
        lamb, laplace = eddy_terms(velocity)
        terms = jnp.einsum(
            "bkpq,bpc->bkqc",
            tiles,
            lamb.reshape(blocks, plane, 3 * depth),
            precision=lax.Precision.HIGHEST,
            preferred_element_type=jnp.float32,
        )
        own = terms[:, 0].reshape(bricks, 2, plane, terms.shape[3]).sum(axis=1)
        spread = jnp.einsum("bs,bqc->sqc", onehot, terms[:, 1], precision=lax.Precision.HIGHEST)
        own, lower, upper = (own + spread[1:-1], spread[0], spread[-1])
        from_upper = shifted(lower, "gx", -1)
        from_lower = shifted(upper, "gx", 1)
        sources.append(attach(own, from_lower, from_upper).reshape(wave_x, width_y, 3, depth))
        if step + 1 < STEPS:
            velocity = velocity + eddy_step * (viscosity * laplace - lamb)
    state = acoustic_state
    for source in sources:
        first = rate(shallow_rim(state), mean_mach, source)
        middle = state + wave_step * first
        second = rate(shallow_rim(middle), mean_mach, source)
        updated = state + 0.5 * wave_step * (first + second)
        state = smooth(shallow_rim(updated))
    return state


def solution(mesh):
    placed = (
        P("gx", "gy", None, "grp"),
        P("gx", "gy"),
        P("gx", "gy", None, None, None),
        P("gx"),
        P("gx", "gy", None, "grp"),
    )
    return jax.shard_map(
        body, mesh=mesh, in_specs=placed, out_specs=P("gx", "gy", None, "grp"), check_vma=False
    )
```

profile of v0, /device:TPU:96, one launch (start us, length us, event | category | flops | bytes accessed | tf_op | source)
XLA Modules:
  0.0 462.9 jit_solution(11736558431419409630)
XLA Ops:
  17.0 7.2 %collective-permute-start.8 = (f32[1,16,3,258]{3,1,2,0:T(8,128)S(1)}, f32[1,16,3,258]{3,1,2,0:T(8,128)S(1)}, u32[]{:S(2)}, u32[]{:S(2)}) collective-permute-start(f32[1,16,3,258]{3,1,2,0:T(8,128)S(1)} %get-tuple-element.82), channel_id=1, source_target_pairs={{2,0},{4,2},{6,4},{8,6},{10,8},{12,10},{14,12},{16,14},{18,16},{20... | collective-permute-start | bytes 148616 | tf_op jit(solution)/shard_map/ppermute | solution.py:26
  28.5 9.6 %collective-permute-start.2 = (f32[3,16,4,262]{3,2,1,0:T(4,128)}, f32[3,16,4,262]{3,2,1,0:T(4,128)}, u32[]{:S(2)}, u32[]{:S(2)}) collective-permute-start(f32[3,16,4,262]{3,2,1,0:T(4,128)} %get-tuple-element.145), channel_id=1, source_target_pairs={{2,0},{4,2},{6,4},{8,6},{10,8},{12,10},{14,12},{16,14},{18,16},{20... | collective-permute-start | bytes 603656 | tf_op jit(solution)/shard_map/ppermute | solution.py:26
  41.3 6.3 %fusion.70 = f32[16,16,4,256]{3,2,1,0:T(4,128)} fusion(f32[16,16,4,256]{3,2,1,0:T(4,128)S(1)} %copy-done, f32[16,16,4,3]{3,2,1,0:T(4,128)} %collective-permute-done, f32[16,16,4,259]{3,2,1,0:T(4,128)S(1)} %constant_dynamic-update-slice_fusion), kind=kLoop, calls=%fused_computation.184 | loop fusion | flops 2883584 | bytes 5255168 | tf_op jit(solution)/shard_map/add | solution.py:77
  54.8 4.5 collective-permute-done.11
  97.2 9.9 %collective-permute-start.13 = (f32[64,768]{1,0:T(8,128)}, f32[64,768]{1,0:T(8,128)}, u32[]{:S(2)}, u32[]{:S(2)}) collective-permute-start(f32[64,768]{1,0:T(8,128)} %bitcast.47), channel_id=1, source_target_pairs={{2,0},{4,2},{6,4},{8,6},{10,8},{12,10},{14,12},{16,14},{18,16},{20... | collective-permute-start | bytes 589832 | tf_op jit(solution)/shard_map/ppermute | solution.py:34
  109.6 3.9 collective-permute-start.34
  120.3 4.4 pad_maximum_fusion.6
  124.7 4.7 %broadcast_multiply_fusion.3 = (f32[16,16,4,256]{3,2,1,0:T(4,128)}, f32[16,16,4,256]{3,2,1,0:T(4,128)}) fusion(f32[16,16]{1,0:T(8,128)S(1)} %copy-done.31, f32[19,16,4,262]{3,2,1,0:T(4,128)S(1)} %get-tuple-element.144, f32[19,16,4,262]{3,2,1,0:T(4,128)S(1)} %get-tuple-element.143), kind=kLoop, calls=%fused_computation.338 | loop fusion | flops 2359296 | bytes 8389632 | tf_op jit(solution)/shard_map/mul | solution.py:83
  136.5 4.3 collective-permute-done.37
  157.9 8.3 %pad_maximum_fusion = (f32[22,19,4,262]{3,2,1,0:T(4,128)S(1)}, f32[22,19,4,262]{3,2,1,0:T(4,128)S(1)}) fusion(f32[22,3,4,262]{3,2,1,0:T(4,128)} %collective-permute-done.4, f32[3,16,4,262]{3,2,1,0:T(4,128)} %collective-permute-done.2, f32[16,16,4,3]{3,2,1,0:T(4,128)} %collective-permute-done.1, f32[16,16,4,256]{3,2,1,0:T(4,128)S(1)} %copy-done, ...), kind=kLoop, calls=%fused_computation | loop fusion | flops 4380640 | bytes 5533440 | tf_op jit(solution)/shard_map/concatenate | solution.py:27
  178.3 10.0 %collective-permute-start.39 = (f32[64,768]{1,0:T(8,128)S(1)}, f32[64,768]{1,0:T(8,128)S(1)}, u32[]{:S(2)}, u32[]{:S(2)}) collective-permute-start(f32[64,768]{1,0:T(8,128)S(1)} %bitcast.57), channel_id=1, source_target_pairs={{2,0},{4,2},{6,4},{8,6},{10,8},{12,10},{14,12},{16,14},{18,16},{20... | collective-permute-start | bytes 589832 | tf_op jit(solution)/shard_map/ppermute | solution.py:34
  194.7 5.6 %fusion.60 = f32[16,16,4,256]{3,2,1,0:T(4,128)S(1)} fusion(f32[16,16,4,256]{3,2,1,0:T(4,128)S(1)} %multiply_add_fusion.2, f32[16,16,4,3]{3,2,1,0:T(4,128)S(1)} %collective-permute-done.14, f32[16,16,4,3]{3,2,1,0:T(4,128)S(1)} %collective-permute-done.15), kind=kLoop, calls=%fused_computation.174 | loop fusion | flops 3670016 | bytes 2121728 | tf_op jit(solution)/shard_map/add | solution.py:77
  200.5 9.1 %collective-permute-done.17 = f32[3,16,4,262]{3,2,1,0:T(4,128)S(1)} collective-permute-done((f32[3,16,4,262]{3,2,1,0:T(4,128)S(1)}, f32[3,16,4,262]{3,2,1,0:T(4,128)S(1)}, u32[]{:S(2)}, u32[]{:S(2)}) %collective-permute-start.17) | collective-permute-done | bytes 201248 | tf_op jit(solution)/shard_map/ppermute | solution.py:23
  220.0 4.1 collective-permute-done.19
  224.1 6.7 %pad_maximum_fusion.1 = (f32[22,19,4,262]{3,2,1,0:T(4,128)S(1)}, f32[22,19,4,262]{3,2,1,0:T(4,128)S(1)}) fusion(f32[22,3,4,262]{3,2,1,0:T(4,128)S(1)} %collective-permute-done.18, f32[3,16,4,262]{3,2,1,0:T(4,128)S(1)} %collective-permute-done.16, f32[16,16,4,3]{3,2,1,0:T(4,128)S(1)} %collective-permute-done.15, f32[16,16,4,256]{3,2,1,0:T(4,128)S(1)} %multiply_add_fusion.2, ...), kind=kLoop, calls=%fused_computation.2 | loop fusion | flops 4380640 | bytes 5533440 | tf_op jit(solution)/shard_map/concatenate | solution.py:27
  255.5 7.7 %collective-permute-done.23 = f32[3,16,4,262]{3,2,1,0:T(4,128)S(1)} collective-permute-done((f32[3,16,4,262]{3,2,1,0:T(4,128)S(1)}, f32[3,16,4,262]{3,2,1,0:T(4,128)S(1)}, u32[]{:S(2)}, u32[]{:S(2)}) %collective-permute-start.23) | collective-permute-done | bytes 201248 | tf_op jit(solution)/shard_map/ppermute | solution.py:23
  273.3 4.1 collective-permute-done.25
  277.4 6.7 %pad_maximum_fusion.2 = (f32[22,19,4,262]{3,2,1,0:T(4,128)S(1)}, f32[22,19,4,262]{3,2,1,0:T(4,128)S(1)}) fusion(f32[22,3,4,262]{3,2,1,0:T(4,128)S(1)} %collective-permute-done.24, f32[3,16,4,262]{3,2,1,0:T(4,128)S(1)} %collective-permute-done.22, f32[16,16,4,3]{3,2,1,0:T(4,128)S(1)} %collective-permute-done.21, f32[16,16,4,256]{3,2,1,0:T(4,128)S(1)} %fusion.151, ...), kind=kLoop, calls=%fused_computation.4 | loop fusion | flops 4380640 | bytes 5533440 | tf_op jit(solution)/shard_map/concatenate | solution.py:27
  284.1 11.9 %fusion.49 = f32[16,16,4,256]{3,2,1,0:T(4,128)S(1)} fusion(f32[16,16,4,256]{3,2,1,0:T(4,128)S(1)} %fusion.151, f32[16,16,4,3]{3,2,1,0:T(4,128)S(1)} %collective-permute-done.20, f32[16,16,4,3]{3,2,1,0:T(4,128)S(1)} %collective-permute-done.21, f32[22,19,4,262]{3,2,1,0:T(4,128)S(1)} %get-tuple-element.96, f32[22,19,4,262]{3,2,1,0:T(4,128)S(1)} %get-tuple-element.95, ...), kind=kLoop, calls=%fused_computation.163 | loop fusion | flops 9437184 | bytes 14704640 | tf_op jit(solution)/shard_map/sub | solution.py:99
  309.6 5.2 %fusion.37 = f32[16,16,4,256]{3,2,1,0:T(4,128)S(1)} fusion(f32[16,16,4,256]{3,2,1,0:T(4,128)S(1)} %fusion.49, f32[16,16,4,3]{3,2,1,0:T(4,128)S(1)} %collective-permute-done.26, f32[16,16,4,3]{3,2,1,0:T(4,128)S(1)} %collective-permute-done.27), kind=kLoop, calls=%fused_computation.151 | loop fusion | flops 3670016 | bytes 2121728 | tf_op jit(solution)/shard_map/add | solution.py:77
  315.3 7.7 %collective-permute-done.29 = f32[3,16,4,262]{3,2,1,0:T(4,128)S(1)} collective-permute-done((f32[3,16,4,262]{3,2,1,0:T(4,128)S(1)}, f32[3,16,4,262]{3,2,1,0:T(4,128)S(1)}, u32[]{:S(2)}, u32[]{:S(2)}) %collective-permute-start.29) | collective-permute-done | bytes 201248 | tf_op jit(solution)/shard_map/ppermute | solution.py:23
  333.9 4.1 collective-permute-done.31
  338.1 6.7 %pad_maximum_fusion.3 = (f32[22,19,4,262]{3,2,1,0:T(4,128)S(1)}, f32[22,19,4,262]{3,2,1,0:T(4,128)S(1)}) fusion(f32[22,3,4,262]{3,2,1,0:T(4,128)S(1)} %collective-permute-done.30, f32[3,16,4,262]{3,2,1,0:T(4,128)S(1)} %collective-permute-done.28, f32[16,16,4,3]{3,2,1,0:T(4,128)S(1)} %collective-permute-done.27, f32[16,16,4,256]{3,2,1,0:T(4,128)S(1)} %fusion.49, ...), kind=kLoop, calls=%fused_computation.6 | loop fusion | flops 4380640 | bytes 5533440 | tf_op jit(solution)/shard_map/concatenate | solution.py:27
  363.2 5.3 %fusion.27 = f32[16,16,4,256]{3,2,1,0:T(4,128)S(1)} fusion(f32[16,16,4,256]{3,2,1,0:T(4,128)S(1)} %multiply_add_fusion.1, f32[16,16,4,3]{3,2,1,0:T(4,128)S(1)} %collective-permute-done.40, f32[16,16,4,3]{3,2,1,0:T(4,128)S(1)} %collective-permute-done.41), kind=kLoop, calls=%fused_computation.141 | loop fusion | flops 3670016 | bytes 2121728 | tf_op jit(solution)/shard_map/add | solution.py:77
  368.5 7.4 %collective-permute-done.43 = f32[3,16,4,262]{3,2,1,0:T(4,128)S(1)} collective-permute-done((f32[3,16,4,262]{3,2,1,0:T(4,128)S(1)}, f32[3,16,4,262]{3,2,1,0:T(4,128)S(1)}, u32[]{:S(2)}, u32[]{:S(2)}) %collective-permute-start.43) | collective-permute-done | bytes 201248 | tf_op jit(solution)/shard_map/ppermute | solution.py:23
  386.0 4.1 collective-permute-done.45
  390.1 6.7 %pad_maximum_fusion.4 = (f32[22,19,4,262]{3,2,1,0:T(4,128)S(1)}, f32[22,19,4,262]{3,2,1,0:T(4,128)S(1)}) fusion(f32[22,3,4,262]{3,2,1,0:T(4,128)S(1)} %collective-permute-done.44, f32[3,16,4,262]{3,2,1,0:T(4,128)S(1)} %collective-permute-done.42, f32[16,16,4,3]{3,2,1,0:T(4,128)S(1)} %collective-permute-done.41, f32[16,16,4,256]{3,2,1,0:T(4,128)S(1)} %multiply_add_fusion.1, ...), kind=kLoop, calls=%fused_computation.8 | loop fusion | flops 4380640 | bytes 5533440 | tf_op jit(solution)/shard_map/concatenate | solution.py:27
  416.4 5.1 %collective-permute-done.48 = f32[3,16,4,262]{3,2,1,0:T(4,128)S(1)} collective-permute-done((f32[3,16,4,262]{3,2,1,0:T(4,128)S(1)}, f32[3,16,4,262]{3,2,1,0:T(4,128)S(1)}, u32[]{:S(2)}, u32[]{:S(2)}) %collective-permute-start.48) | collective-permute-done | bytes 201248 | tf_op jit(solution)/shard_map/ppermute | solution.py:26
  421.5 7.7 %collective-permute-done.49 = f32[3,16,4,262]{3,2,1,0:T(4,128)S(1)} collective-permute-done((f32[3,16,4,262]{3,2,1,0:T(4,128)S(1)}, f32[3,16,4,262]{3,2,1,0:T(4,128)S(1)}, u32[]{:S(2)}, u32[]{:S(2)}) %collective-permute-start.49) | collective-permute-done | bytes 201248 | tf_op jit(solution)/shard_map/ppermute | solution.py:23
  439.2 4.1 collective-permute-done.51
  443.3 6.7 %pad_maximum_fusion.5 = (f32[22,19,4,262]{3,2,1,0:T(4,128)S(1)}, f32[22,19,4,262]{3,2,1,0:T(4,128)S(1)}) fusion(f32[22,3,4,262]{3,2,1,0:T(4,128)S(1)} %collective-permute-done.50, f32[3,16,4,262]{3,2,1,0:T(4,128)S(1)} %collective-permute-done.48, f32[16,16,4,3]{3,2,1,0:T(4,128)S(1)} %collective-permute-done.47, f32[16,16,4,256]{3,2,1,0:T(4,128)S(1)} %fusion.153, ...), kind=kLoop, calls=%fused_computation.10 | loop fusion | flops 4380640 | bytes 5533440 | tf_op jit(solution)/shard_map/concatenate | solution.py:27
  450.0 12.6 %fusion.16 = f32[16,16,4,256]{3,2,1,0:T(4,128)} fusion(f32[16,16,4,256]{3,2,1,0:T(4,128)S(1)} %fusion.153, f32[16,16,4,3]{3,2,1,0:T(4,128)S(1)} %collective-permute-done.46, f32[16,16,4,3]{3,2,1,0:T(4,128)S(1)} %collective-permute-done.47, f32[22,19,4,262]{3,2,1,0:T(4,128)S(1)} %get-tuple-element.84, f32[22,19,4,262]{3,2,1,0:T(4,128)S(1)} %get-tuple-element.83, ...), kind=kLoop, calls=%fused_computation.130 | loop fusion | flops 9437184 | bytes 14704640 | tf_op jit(solution)/shard_map/sub | solution.py:99
  (257 shorter events, 248.5 us)
Async XLA Ops:
  2.1 12.3 %collective-permute-start.6 = (f32[32,16,3,1]{0,1,3,2:T(8,128)S(1)}, f32[32,16,3,1]{0,1,3,2:T(8,128)S(1)}, u32[]{:S(2)}, u32[]{:S(2)}) collective-permute-start(f32[32,16,3,1]{0,1,3,2:T(8,128)S(1)} %copy.88), channel_id=1, source_target_pairs={{64,0},{65,1},{66,2},{67,3},{68,4},{69,5},{70,6},{71,7},{72,8},{73... | collective-permute-start | bytes 18440 | tf_op jit(solution)/shard_map/ppermute | solution.py:26
  3.8 11.0 %collective-permute-start.7 = (f32[32,16,3,1]{0,1,3,2:T(8,128)S(1)}, f32[32,16,3,1]{0,1,3,2:T(8,128)S(1)}, u32[]{:S(2)}, u32[]{:S(2)}) collective-permute-start(f32[32,16,3,1]{0,1,3,2:T(8,128)S(1)} %copy.89), channel_id=1, source_target_pairs={{0,64},{1,65},{2,66},{3,67},{4,68},{5,69},{6,70},{7,71},{8,72},{9,... | collective-permute-start | bytes 18440 | tf_op jit(solution)/shard_map/ppermute | solution.py:23
  8.3 17.9 %collective-permute-start = (f32[16,16,4,3]{3,2,1,0:T(4,128)}, f32[16,16,4,3]{3,2,1,0:T(4,128)}, u32[]{:S(2)}, u32[]{:S(2)}) collective-permute-start(f32[16,16,4,3]{3,2,1,0:T(4,128)} %get-tuple-element.166), channel_id=1, source_target_pairs={{0,64},{1,65},{2,66},{3,67},{4,68},{5,69},{6,70},{7,71},{8,72},{9,... | collective-permute-start | bytes 36872 | tf_op jit(solution)/shard_map/ppermute | solution.py:23
  10.4 15.7 %collective-permute-start.1 = (f32[16,16,4,3]{3,2,1,0:T(4,128)}, f32[16,16,4,3]{3,2,1,0:T(4,128)}, u32[]{:S(2)}, u32[]{:S(2)}) collective-permute-start(f32[16,16,4,3]{3,2,1,0:T(4,128)} %get-tuple-element.165), channel_id=1, source_target_pairs={{64,0},{65,1},{66,2},{67,3},{68,4},{69,5},{70,6},{71,7},{72,8},{73... | collective-permute-start | bytes 36872 | tf_op jit(solution)/shard_map/ppermute | solution.py:26
  17.0 30.6 %collective-permute-start.8 = (f32[1,16,3,258]{3,1,2,0:T(8,128)S(1)}, f32[1,16,3,258]{3,1,2,0:T(8,128)S(1)}, u32[]{:S(2)}, u32[]{:S(2)}) collective-permute-start(f32[1,16,3,258]{3,1,2,0:T(8,128)S(1)} %get-tuple-element.82), channel_id=1, source_target_pairs={{2,0},{4,2},{6,4},{8,6},{10,8},{12,10},{14,12},{16,14},{18,16},{20... | collective-permute-start | bytes 148616 | tf_op jit(solution)/shard_map/ppermute | solution.py:26
  24.2 23.4 %collective-permute-start.9 = (f32[1,16,3,258]{3,1,2,0:T(8,128)S(1)}, f32[1,16,3,258]{3,1,2,0:T(8,128)S(1)}, u32[]{:S(2)}, u32[]{:S(2)}) collective-permute-start(f32[1,16,3,258]{3,1,2,0:T(8,128)S(1)} %get-tuple-element.81), channel_id=1, source_target_pairs={{0,2},{2,4},{4,6},{6,8},{8,10},{10,12},{12,14},{14,16},{16,18},{18... | collective-permute-start | bytes 148616 | tf_op jit(solution)/shard_map/ppermute | solution.py:23
  28.5 85.0 %collective-permute-start.2 = (f32[3,16,4,262]{3,2,1,0:T(4,128)}, f32[3,16,4,262]{3,2,1,0:T(4,128)}, u32[]{:S(2)}, u32[]{:S(2)}) collective-permute-start(f32[3,16,4,262]{3,2,1,0:T(4,128)} %get-tuple-element.145), channel_id=1, source_target_pairs={{2,0},{4,2},{6,4},{8,6},{10,8},{12,10},{14,12},{16,14},{18,16},{20... | collective-permute-start | bytes 603656 | tf_op jit(solution)/shard_map/ppermute | solution.py:26
  38.2 77.3 %collective-permute-start.3 = (f32[3,16,4,262]{3,2,1,0:T(4,128)}, f32[3,16,4,262]{3,2,1,0:T(4,128)}, u32[]{:S(2)}, u32[]{:S(2)}) collective-permute-start(f32[3,16,4,262]{3,2,1,0:T(4,128)} %get-tuple-element.146), channel_id=1, source_target_pairs={{0,2},{2,4},{4,6},{6,8},{8,10},{10,12},{12,14},{14,16},{16,18},{18... | collective-permute-start | bytes 603656 | tf_op jit(solution)/shard_map/ppermute | solution.py:23
  89.2 18.3 %collective-permute-start.33 = (f32[32,16,3,1]{0,1,3,2:T(8,128)S(1)}, f32[32,16,3,1]{0,1,3,2:T(8,128)S(1)}, u32[]{:S(2)}, u32[]{:S(2)}) collective-permute-start(f32[32,16,3,1]{0,1,3,2:T(8,128)S(1)} %copy.73), channel_id=1, source_target_pairs={{0,64},{1,65},{2,66},{3,67},{4,68},{5,69},{6,70},{7,71},{8,72},{9,... | collective-permute-start | bytes 18440 | tf_op jit(solution)/shard_map/ppermute | solution.py:23
  93.1 62.2 %collective-permute-start.12 = (f32[64,768]{1,0:T(8,128)}, f32[64,768]{1,0:T(8,128)}, u32[]{:S(2)}, u32[]{:S(2)}) collective-permute-start(f32[64,768]{1,0:T(8,128)} %bitcast.45), channel_id=1, source_target_pairs={{0,2},{2,4},{4,6},{6,8},{8,10},{10,12},{12,14},{14,16},{16,18},{18... | collective-permute-start | bytes 589832 | tf_op jit(solution)/shard_map/ppermute | solution.py:34
  97.2 59.3 %collective-permute-start.13 = (f32[64,768]{1,0:T(8,128)}, f32[64,768]{1,0:T(8,128)}, u32[]{:S(2)}, u32[]{:S(2)}) collective-permute-start(f32[64,768]{1,0:T(8,128)} %bitcast.47), channel_id=1, source_target_pairs={{2,0},{4,2},{6,4},{8,6},{10,8},{12,10},{14,12},{16,14},{18,16},{20... | collective-permute-start | bytes 589832 | tf_op jit(solution)/shard_map/ppermute | solution.py:34
  109.6 19.7 %collective-permute-start.34 = (f32[1,16,3,258]{3,1,2,0:T(8,128)S(1)}, f32[1,16,3,258]{3,1,2,0:T(8,128)S(1)}, u32[]{:S(2)}, u32[]{:S(2)}) collective-permute-start(f32[1,16,3,258]{3,1,2,0:T(8,128)S(1)} %get-tuple-element.75), channel_id=1, source_target_pairs={{2,0},{4,2},{6,4},{8,6},{10,8},{12,10},{14,12},{16,14},{18,16},{20... | collective-permute-start | bytes 148616 | tf_op jit(solution)/shard_map/ppermute | solution.py:26
  113.6 15.8 %collective-permute-start.35 = (f32[1,16,3,258]{3,1,2,0:T(8,128)S(1)}, f32[1,16,3,258]{3,1,2,0:T(8,128)S(1)}, u32[]{:S(2)}, u32[]{:S(2)}) collective-permute-start(f32[1,16,3,258]{3,1,2,0:T(8,128)S(1)} %get-tuple-element.76), channel_id=1, source_target_pairs={{0,2},{2,4},{4,6},{6,8},{8,10},{10,12},{12,14},{14,16},{16,18},{18... | collective-permute-start | bytes 148616 | tf_op jit(solution)/shard_map/ppermute | solution.py:23
  118.1 39.8 %collective-permute-start.4 = (f32[22,3,4,262]{3,2,1,0:T(4,128)}, f32[22,3,4,262]{3,2,1,0:T(4,128)}, u32[]{:S(2)}, u32[]{:S(2)}) collective-permute-start(f32[22,3,4,262]{3,2,1,0:T(4,128)} %get-tuple-element.105), channel_id=1, source_target_pairs={{1,0},{3,2},{5,4},{7,6},{9,8},{11,10},{13,12},{15,14},{17,16},{19,... | collective-permute-start | bytes 830024 | tf_op jit(solution)/shard_map/ppermute | solution.py:26
  134.6 23.3 %collective-permute-start.5 = (f32[22,3,4,262]{3,2,1,0:T(4,128)}, f32[22,3,4,262]{3,2,1,0:T(4,128)}, u32[]{:S(2)}, u32[]{:S(2)}) collective-permute-start(f32[22,3,4,262]{3,2,1,0:T(4,128)} %get-tuple-element.106), channel_id=1, source_target_pairs={{0,1},{2,3},{4,5},{6,7},{8,9},{10,11},{12,13},{14,15},{16,17},{18,... | collective-permute-start | bytes 830024 | tf_op jit(solution)/shard_map/ppermute | solution.py:23
  173.3 15.1 %collective-permute-start.14 = (f32[16,16,4,3]{3,2,1,0:T(4,128)S(1)}, f32[16,16,4,3]{3,2,1,0:T(4,128)S(1)}, u32[]{:S(2)}, u32[]{:S(2)}) collective-permute-start(f32[16,16,4,3]{3,2,1,0:T(4,128)S(1)} %get-tuple-element.164), channel_id=1, source_target_pairs={{0,64},{1,65},{2,66},{3,67},{4,68},{5,69},{6,70},{7,71},{8,72},{9,... | collective-permute-start | bytes 36872 | tf_op jit(solution)/shard_map/ppermute | solution.py:23
  174.7 13.6 %collective-permute-start.15 = (f32[16,16,4,3]{3,2,1,0:T(4,128)S(1)}, f32[16,16,4,3]{3,2,1,0:T(4,128)S(1)}, u32[]{:S(2)}, u32[]{:S(2)}) collective-permute-start(f32[16,16,4,3]{3,2,1,0:T(4,128)S(1)} %get-tuple-element.163), channel_id=1, source_target_pairs={{64,0},{65,1},{66,2},{67,3},{68,4},{69,5},{70,6},{71,7},{72,8},{73... | collective-permute-start | bytes 36872 | tf_op jit(solution)/shard_map/ppermute | solution.py:26
  176.4 74.0 %collective-permute-start.38 = (f32[64,768]{1,0:T(8,128)S(1)}, f32[64,768]{1,0:T(8,128)S(1)}, u32[]{:S(2)}, u32[]{:S(2)}) collective-permute-start(f32[64,768]{1,0:T(8,128)S(1)} %bitcast.58), channel_id=1, source_target_pairs={{0,2},{2,4},{4,6},{6,8},{8,10},{10,12},{12,14},{14,16},{16,18},{18... | collective-permute-start | bytes 589832 | tf_op jit(solution)/shard_map/ppermute | solution.py:34
  178.3 121.7 %collective-permute-start.39 = (f32[64,768]{1,0:T(8,128)S(1)}, f32[64,768]{1,0:T(8,128)S(1)}, u32[]{:S(2)}, u32[]{:S(2)}) collective-permute-start(f32[64,768]{1,0:T(8,128)S(1)} %bitcast.57), channel_id=1, source_target_pairs={{2,0},{4,2},{6,4},{8,6},{10,8},{12,10},{14,12},{16,14},{18,16},{20... | collective-permute-start | bytes 589832 | tf_op jit(solution)/shard_map/ppermute | solution.py:34
  188.8 11.7 %collective-permute-start.16 = (f32[3,16,4,262]{3,2,1,0:T(4,128)S(1)}, f32[3,16,4,262]{3,2,1,0:T(4,128)S(1)}, u32[]{:S(2)}, u32[]{:S(2)}) collective-permute-start(f32[3,16,4,262]{3,2,1,0:T(4,128)S(1)} %get-tuple-element.137), channel_id=1, source_target_pairs={{2,0},{4,2},{6,4},{8,6},{10,8},{12,10},{14,12},{16,14},{18,16},{20... | collective-permute-start | bytes 603656 | tf_op jit(solution)/shard_map/ppermute | solution.py:26
  192.8 16.8 %collective-permute-start.17 = (f32[3,16,4,262]{3,2,1,0:T(4,128)S(1)}, f32[3,16,4,262]{3,2,1,0:T(4,128)S(1)}, u32[]{:S(2)}, u32[]{:S(2)}) collective-permute-start(f32[3,16,4,262]{3,2,1,0:T(4,128)S(1)} %get-tuple-element.138), channel_id=1, source_target_pairs={{0,2},{2,4},{4,6},{6,8},{8,10},{10,12},{12,14},{14,16},{16,18},{18... | collective-permute-start | bytes 603656 | tf_op jit(solution)/shard_map/ppermute | solution.py:23
  211.4 12.7 %collective-permute-start.19 = (f32[22,3,4,262]{3,2,1,0:T(4,128)S(1)}, f32[22,3,4,262]{3,2,1,0:T(4,128)S(1)}, u32[]{:S(2)}, u32[]{:S(2)}) collective-permute-start(f32[22,3,4,262]{3,2,1,0:T(4,128)S(1)} %get-tuple-element.102), channel_id=1, source_target_pairs={{0,1},{2,3},{4,5},{6,7},{8,9},{10,11},{12,13},{14,15},{16,17},{18,... | collective-permute-start | bytes 830024 | tf_op jit(solution)/shard_map/ppermute | solution.py:23
  246.5 16.7 %collective-permute-start.23 = (f32[3,16,4,262]{3,2,1,0:T(4,128)S(1)}, f32[3,16,4,262]{3,2,1,0:T(4,128)S(1)}, u32[]{:S(2)}, u32[]{:S(2)}) collective-permute-start(f32[3,16,4,262]{3,2,1,0:T(4,128)S(1)} %get-tuple-element.129), channel_id=1, source_target_pairs={{0,2},{2,4},{4,6},{6,8},{8,10},{10,12},{12,14},{14,16},{16,18},{18... | collective-permute-start | bytes 603656 | tf_op jit(solution)/shard_map/ppermute | solution.py:23
  265.1 12.3 %collective-permute-start.25 = (f32[22,3,4,262]{3,2,1,0:T(4,128)S(1)}, f32[22,3,4,262]{3,2,1,0:T(4,128)S(1)}, u32[]{:S(2)}, u32[]{:S(2)}) collective-permute-start(f32[22,3,4,262]{3,2,1,0:T(4,128)S(1)} %get-tuple-element.98), channel_id=1, source_target_pairs={{0,1},{2,3},{4,5},{6,7},{8,9},{10,11},{12,13},{14,15},{16,17},{18,... | collective-permute-start | bytes 830024 | tf_op jit(solution)/shard_map/ppermute | solution.py:23
  303.7 11.6 %collective-permute-start.28 = (f32[3,16,4,262]{3,2,1,0:T(4,128)S(1)}, f32[3,16,4,262]{3,2,1,0:T(4,128)S(1)}, u32[]{:S(2)}, u32[]{:S(2)}) collective-permute-start(f32[3,16,4,262]{3,2,1,0:T(4,128)S(1)} %get-tuple-element.125), channel_id=1, source_target_pairs={{2,0},{4,2},{6,4},{8,6},{10,8},{12,10},{14,12},{16,14},{18,16},{20... | collective-permute-start | bytes 603656 | tf_op jit(solution)/shard_map/ppermute | solution.py:26
  305.7 17.3 %collective-permute-start.29 = (f32[3,16,4,262]{3,2,1,0:T(4,128)S(1)}, f32[3,16,4,262]{3,2,1,0:T(4,128)S(1)}, u32[]{:S(2)}, u32[]{:S(2)}) collective-permute-start(f32[3,16,4,262]{3,2,1,0:T(4,128)S(1)} %get-tuple-element.126), channel_id=1, source_target_pairs={{0,2},{2,4},{4,6},{6,8},{8,10},{10,12},{12,14},{14,16},{16,18},{18... | collective-permute-start | bytes 603656 | tf_op jit(solution)/shard_map/ppermute | solution.py:23
  324.9 13.2 %collective-permute-start.31 = (f32[22,3,4,262]{3,2,1,0:T(4,128)S(1)}, f32[22,3,4,262]{3,2,1,0:T(4,128)S(1)}, u32[]{:S(2)}, u32[]{:S(2)}) collective-permute-start(f32[22,3,4,262]{3,2,1,0:T(4,128)S(1)} %get-tuple-element.94), channel_id=1, source_target_pairs={{0,1},{2,3},{4,5},{6,7},{8,9},{10,11},{12,13},{14,15},{16,17},{18,... | collective-permute-start | bytes 830024 | tf_op jit(solution)/shard_map/ppermute | solution.py:23
  357.3 11.2 %collective-permute-start.42 = (f32[3,16,4,262]{3,2,1,0:T(4,128)S(1)}, f32[3,16,4,262]{3,2,1,0:T(4,128)S(1)}, u32[]{:S(2)}, u32[]{:S(2)}) collective-permute-start(f32[3,16,4,262]{3,2,1,0:T(4,128)S(1)} %get-tuple-element.117), channel_id=1, source_target_pairs={{2,0},{4,2},{6,4},{8,6},{10,8},{12,10},{14,12},{16,14},{18,16},{20... | collective-permute-start | bytes 603656 | tf_op jit(solution)/shard_map/ppermute | solution.py:26
  359.5 16.5 %collective-permute-start.43 = (f32[3,16,4,262]{3,2,1,0:T(4,128)S(1)}, f32[3,16,4,262]{3,2,1,0:T(4,128)S(1)}, u32[]{:S(2)}, u32[]{:S(2)}) collective-permute-start(f32[3,16,4,262]{3,2,1,0:T(4,128)S(1)} %get-tuple-element.118), channel_id=1, source_target_pairs={{0,2},{2,4},{4,6},{6,8},{8,10},{10,12},{12,14},{14,16},{16,18},{18... | collective-permute-start | bytes 603656 | tf_op jit(solution)/shard_map/ppermute | solution.py:23
  377.9 12.2 %collective-permute-start.45 = (f32[22,3,4,262]{3,2,1,0:T(4,128)S(1)}, f32[22,3,4,262]{3,2,1,0:T(4,128)S(1)}, u32[]{:S(2)}, u32[]{:S(2)}) collective-permute-start(f32[22,3,4,262]{3,2,1,0:T(4,128)S(1)} %get-tuple-element.90), channel_id=1, source_target_pairs={{0,1},{2,3},{4,5},{6,7},{8,9},{10,11},{12,13},{14,15},{16,17},{18,... | collective-permute-start | bytes 830024 | tf_op jit(solution)/shard_map/ppermute | solution.py:23
  412.6 16.5 %collective-permute-start.49 = (f32[3,16,4,262]{3,2,1,0:T(4,128)S(1)}, f32[3,16,4,262]{3,2,1,0:T(4,128)S(1)}, u32[]{:S(2)}, u32[]{:S(2)}) collective-permute-start(f32[3,16,4,262]{3,2,1,0:T(4,128)S(1)} %get-tuple-element.109), channel_id=1, source_target_pairs={{0,2},{2,4},{4,6},{6,8},{8,10},{10,12},{12,14},{14,16},{16,18},{18... | collective-permute-start | bytes 603656 | tf_op jit(solution)/shard_map/ppermute | solution.py:23
  431.1 12.2 %collective-permute-start.51 = (f32[22,3,4,262]{3,2,1,0:T(4,128)S(1)}, f32[22,3,4,262]{3,2,1,0:T(4,128)S(1)}, u32[]{:S(2)}, u32[]{:S(2)}) collective-permute-start(f32[22,3,4,262]{3,2,1,0:T(4,128)S(1)} %get-tuple-element.86), channel_id=1, source_target_pairs={{0,1},{2,3},{4,5},{6,7},{8,9},{10,11},{12,13},{14,15},{16,17},{18,... | collective-permute-start | bytes 830024 | tf_op jit(solution)/shard_map/ppermute | solution.py:23
  (55 other events, 312.5 us)
where the time goes:
time: 470 us; the launch traced here: 463 us
  other arithmetic  188 us (40%)
  starting transfers between devices  128 us (27%)
  waiting for transfers between devices  97.2 us (21%)
  local copies, waits for them, and re-layouts  38 us (8%)
  matrix products  9.11 us (2%)
    ppermute x24, waiting for transfers between devices, padded_2(): lax.ppermute(lax.slice_in_dim(block, block.shape[dim] - width, None, axis...  69.4 us
    concatenate x16, other arithmetic, padded_2(): block = jnp.concatenate([low, block, high], axis=dim)  64.6 us
    ppermute x24, starting transfers between devices, padded_2(): lax.ppermute(lax.slice_in_dim(block, 0, width, axis=dim), axis, backward)  55.3 us
    ppermute x24, starting transfers between devices, padded_2(): lax.ppermute(lax.slice_in_dim(block, block.shape[dim] - width, None, axis...  49.1 us
    add x8, other arithmetic, derivative(): total = term if total is None else total + term  35.6 us
    ppermute x24, waiting for transfers between devices, padded_2(): lax.ppermute(lax.slice_in_dim(block, 0, width, axis=dim), axis, backward)  27.8 us
    sub x2, other arithmetic, smooth(): return center - filter_weight * total  24.6 us
    ppermute x4, starting transfers between devices, shifted(): return lax.ppermute(array, axis, pairs)  24.1 us
  transfers between devices with their start and end apart: 52, of which 27 were waited for; matrix products, arithmetic and copies ran while one was open for 36% of the time, Pallas kernels for 0%

commit v1 on v0

v1 whole, which is shorter than its diff:
```python
import functools

import jax
import jax.numpy as jnp
from jax import lax
from jax.experimental import pallas as pl
from jax.experimental.pallas import tpu as pltpu
from jax.sharding import PartitionSpec as P

MESH = pl.DeviceIdType.MESH
F32, BF16 = jnp.float32, jnp.bfloat16

eddy_step = 0.1
viscosity = 0.5
wave_step = 0.2
filter_weight = 0.2
derivative_weights = (0.770882380518, -0.166705904415, 0.02084314277)
filter_taps = (0.28739284246, -0.226146951809, 0.10630357877, -0.023853048191)

NX, NA, NY, L = 32, 16, 16, 128
R0 = 8
EX = 3
STAGES = 6
ROWS = pl.ds(R0, NY)


def kernel(count, les, mach, tiles, offs, state, out, v0, v1, zv, f, zf, stage, lb, wk, s, tb, mb, tl, mc,
           send, recv, local):
    ix, iy, ig = lax.axis_index("gx"), lax.axis_index("gy"), lax.axis_index("grp")
    has_l, has_r = ix > 0, ix < count - 1
    right = {"gx": jnp.minimum(ix + 1, count - 1)}
    left = {"gx": jnp.maximum(ix - 1, 0)}
    side, twin = {"gy": 1 - iy}, {"grp": 1 - ig}

    loads = []
    for h in range(2):
        loads.append(pltpu.make_async_copy(les.at[:, :, :, pl.ds(L * h, L)], v0.at[pl.ds(1, NX), :, h, ROWS, :], local.at[h]))
    loads.append(pltpu.make_async_copy(state, stage, local.at[2]))
    loads.append(pltpu.make_async_copy(tiles, tl, local.at[3]))
    loads.append(pltpu.make_async_copy(mach, mc, local.at[4]))
    for c in loads:
        c.start()

    def clear(ref):
        def go(x, _):
            @pl.when(iy == 0)
            def _():
                ref[x, :, :, pl.ds(0, 8), :] = jnp.zeros(ref.shape[1:3] + (8, L), F32)
            @pl.when(iy == 1)
            def _():
                ref[x, :, :, pl.ds(24, 8), :] = jnp.zeros(ref.shape[1:3] + (8, L), F32)
            return 0
        lax.fori_loop(0, ref.shape[0], go, 0)

    def clear_x(ref, width):
        n = ref.shape[0]
        @pl.when(jnp.logical_not(has_l))
        def _():
            for x in range(width):
                ref[x, :, :, ROWS, :] = jnp.zeros(ref.shape[1:3] + (NY, L), F32)
        @pl.when(jnp.logical_not(has_r))
        def _():
            for x in range(n - width, n):
                ref[x, :, :, ROWS, :] = jnp.zeros(ref.shape[1:3] + (NY, L), F32)

    bar = pltpu.get_barrier_semaphore()

    @pl.when(has_l)
    def _():
        pl.semaphore_signal(bar, inc=1, device_id=left, device_id_type=MESH)

    @pl.when(has_r)
    def _():
        pl.semaphore_signal(bar, inc=1, device_id=right, device_id_type=MESH)

    pl.semaphore_signal(bar, inc=1, device_id=side, device_id_type=MESH)
    pl.semaphore_signal(bar, inc=1, device_id=twin, device_id_type=MESH)

    for ref, width in ((v0, 1), (v1, 1)):
        clear(ref)
        clear_x(ref, width)
    for n in range(STAGES):
        clear(f.at[n])
        clear_x(f.at[n], EX)
    for n in range(2):
        @pl.when(jnp.logical_not(has_l))
        def _():
            tb[n, 0] = jnp.zeros(tb.shape[2:], F32)
        @pl.when(jnp.logical_not(has_r))
        def _():
            tb[n, 1] = jnp.zeros(tb.shape[2:], F32)

    for c in loads:
        c.wait()

    flow = jnp.transpose(mc[...])
    for x in range(NA):
        mb[x] = jnp.broadcast_to(flow[:, x:x + 1], (NY, L))

    for m in range(-1, 5):
        for j in range(6):
            b = 2 * m - 2 + j
            if not 0 <= b < 8:
                continue
            if j in (2, 3):
                t = tl[b, 0]
            else:
                way = 1.0 if j < 2 else -1.0
                w = 0.5 + 0.5 * way * offs[b].astype(F32)
                t = (tl[b, 1].astype(F32) * w).astype(BF16)
            wk[m + 1, pl.ds(j * 128, 64), :] = t
            wk[m + 1, pl.ds(j * 128 + 64, 64), :] = t

    def relayout(x, _):
        for h in range(2):
            for c in range(4):
                f[0, x + EX, c, h, ROWS, :] = stage[pl.ds(x * 128 + h * 4 + c, NY, stride=8), :]
        return 0

    lax.fori_loop(0, NA, relayout, 0)

    pl.semaphore_wait(bar, 2 + has_l.astype(jnp.int32) + has_r.astype(jnp.int32))

    def remote(k, src, dst, to):
        return pltpu.make_async_remote_copy(src, dst, send.at[k], recv.at[k], device_id=to, device_id_type=MESH)

    class Halo:
        def __init__(self, k, ref, zref, own, width):
            n = ref.shape[0]
            first, last = width, width + own
            self.right = remote(4 * k, ref.at[pl.ds(last - width, width), :, :, ROWS, :],
                                ref.at[pl.ds(0, width), :, :, ROWS, :], right)
            self.left = remote(4 * k + 1, ref.at[pl.ds(first, width), :, :, ROWS, :],
                               ref.at[pl.ds(last, width), :, :, ROWS, :], left)
            src = jnp.where(iy == 0, R0 + NY - width, R0)
            dst = jnp.where(iy == 0, R0 - width, R0 + NY)
            self.side = remote(4 * k + 2, ref.at[pl.ds(first, own), :, :, pl.ds(src, width), :],
                               ref.at[pl.ds(first, own), :, :, pl.ds(dst, width), :], side)
            self.twin = remote(4 * k + 3, ref.at[pl.ds(first, own), :, 1 - ig, ROWS, :], zref, twin)

        def start(self):
            pl.when(has_r)(self.right.start)
            pl.when(has_l)(self.left.start)
            self.side.start()
            self.twin.start()

        def wait(self):
            self.twin.wait_recv()
            self.side.wait_recv()
            pl.when(has_l)(self.right.wait_recv)
            pl.when(has_r)(self.left.wait_recv)

        def drain(self):
            pl.when(has_r)(self.right.wait_send)
            pl.when(has_l)(self.left.wait_send)
            self.side.wait_send()
            self.twin.wait_send()

    halos = [Halo(n, f.at[n], zf.at[n], NA, EX) for n in range(STAGES)]
    eddies = [Halo(STAGES + n, (v0, v1)[n], zv.at[n], NX, 1) for n in range(2)]
    base = 4 * (STAGES + 2)
    terms = [(remote(base + 2 * n, tb.at[n, 3], tb.at[n, 0], right), remote(base + 2 * n + 1, tb.at[n, 2], tb.at[n, 1], left))
             for n in range(2)]

    eddies[0].start()
    halos[0].start()

    lane = lax.broadcasted_iota(jnp.int32, (NY, L), 1)
    keep = (lane >= 64).astype(jnp.int32) == ig

    def ahead(cur, nxt, j):
        return pltpu.roll(jnp.where(lane < j, nxt, cur), L - j, 1)

    def behind(cur, prv, j):
        return pltpu.roll(jnp.where(lane >= L - j, prv, cur), j, 1)

    def eddy(n):
        src, zsrc = (v0, v1)[n], zv.at[n]

        def go(x, _):
            b, i = x // 4, lax.rem(x, 4)
            halves = [[src[x + 1, c, h, ROWS, :] for h in range(2)] for c in range(3)]
            edge = [jnp.where(keep, zsrc[x, c], 0.0) for c in range(3)]
            for h in range(2):
                grads, laps = [], []
                for c in range(3):
                    cen = halves[c][h]
                    xp, xm = src[x + 2, c, h, ROWS, :], src[x, c, h, ROWS, :]
                    yp, ym = src[x + 1, c, h, pl.ds(R0 + 1, NY), :], src[x + 1, c, h, pl.ds(R0 - 1, NY), :]
                    nxt, prv = (halves[c][1], edge[c]) if h == 0 else (edge[c], halves[c][0])
                    zp, zm = ahead(cen, nxt, 1), behind(cen, prv, 1)
                    grads.append((0.5 * (xp - xm), 0.5 * (yp - ym), 0.5 * (zp - zm)))
                    if n == 0:
                        laps.append(((xp + xm) + (yp + ym)) + ((zp + zm) - 6.0 * cen))
                u, v, w = (halves[c][h] for c in range(3))
                ox = grads[2][1] - grads[1][2]
                oy = grads[0][2] - grads[2][0]
                oz = grads[1][0] - grads[0][1]
                lamb = (oy * w - oz * v, oz * u - ox * w, ox * v - oy * u)
                for c in range(3):
                    hi = lamb[c].astype(BF16)
                    lo = (lamb[c] - hi.astype(F32)).astype(BF16)
                    at = pl.multiple_of(b * 128 + i * 16, 16)
                    lb[pl.ds(at, 16), pl.ds((c * 2 + h) * L, L)] = hi
                    lb[pl.ds(at + 64, 16), pl.ds((c * 2 + h) * L, L)] = lo
                    if n == 0:
                        v1[x + 1, c, h, ROWS, :] = halves[c][h] + eddy_step * (viscosity * laps[c] - lamb[c])
            return 0

        lax.fori_loop(0, NX, go, 0)

    def product(m):
        j0, j1 = max(0, 2 - 2 * m), min(6, 10 - 2 * m)
        rows = pl.ds((2 * m - 2 + j0) * 128, (j1 - j0) * 128)
        return lax.dot_general(wk[m + 1, pl.ds(j0 * 128, (j1 - j0) * 128), :], lb[rows, :],
                               (((0,), (0,)), ((), ())), preferred_element_type=F32)

    def restrict(n):
        for m, slot in ((4, 3), (-1, 2)):
            r = product(m)
            for i in range(4):
                for c in range(3):
                    for h in range(2):
                        tb[n, slot, i, c, h] = r[i * 16:(i + 1) * 16, (c * 2 + h) * L:(c * 2 + h + 1) * L]
        pl.when(has_r)(terms[n][0].start)
        pl.when(has_l)(terms[n][1].start)
        for m in range(4):
            r = product(m)
            for i in range(4):
                for c in range(3):
                    for h in range(2):
                        s[n, 4 * m + i, c, h] = r[i * 16:(i + 1) * 16, (c * 2 + h) * L:(c * 2 + h + 1) * L]

    def attach(n):
        pl.when(has_l)(terms[n][0].wait_recv)
        pl.when(has_r)(terms[n][1].wait_recv)
        for i in range(4):
            s[n, i] = s[n, i] + tb[n, 0, i]
            s[n, 12 + i] = s[n, 12 + i] + tb[n, 1, i]

    def slope(ahead_, behind_):
        total = None
        for j in range(3):
            t = derivative_weights[j] * (ahead_[j] - behind_[j])
            total = t if total is None else total + t
        return total

    def rate(n, k, x):
        src, zsrc = f.at[n], zf.at[n]
        halves = [[src[x + EX, c, h, ROWS, :] for h in range(2)] for c in range(4)]
        edge = {c: jnp.where(keep, zsrc[x, c], 0.0) for c in (0, 3)}
        m = mb[x]
        result = []
        for h in range(2):
            def dx(c):
                return slope([src[x + EX + j, c, h, ROWS, :] for j in (1, 2, 3)], [src[x + EX - j, c, h, ROWS, :] for j in (1, 2, 3)])

            def dy(c):
                return slope([src[x + EX, c, h, pl.ds(R0 + j, NY), :] for j in (1, 2, 3)],
                             [src[x + EX, c, h, pl.ds(R0 - j, NY), :] for j in (1, 2, 3)])

            def dz(c):
                cen = halves[c][h]
                nxt, prv = (halves[c][1], edge[c]) if h == 0 else (edge[c], halves[c][0])
                return slope([ahead(cen, nxt, j) for j in (1, 2, 3)], [behind(cen, prv, j) for j in (1, 2, 3)])

            d = [dx(c) for c in range(4)]
            result.append((
                -(m * d[0] + d[1] + dy(2) + dz(3)),
                -(m * d[1] + d[0]) - s[k, x, 0, h],
                -(m * d[2] + dy(0)) - s[k, x, 1, h],
                -(m * d[3] + dz(0)) - s[k, x, 2, h],
            ))
        return halves, result

    def first(n, k):
        def go(x, _):
            cen, r = rate(n, k, x)
            for h in range(2):
                for c in range(4):
                    f[n + 1, x + EX, c, h, ROWS, :] = cen[c][h] + wave_step * r[h][c]
            return 0
        lax.fori_loop(0, NA, go, 0)

    def second(n, k):
        def go(x, _):
            cen, r = rate(n, k, x)
            for h in range(2):
                for c in range(4):
                    f[n + 1, x + EX, c, h, ROWS, :] = (0.5 * (f[n - 1, x + EX, c, h, ROWS, :] + cen[c][h])
                                                       + 0.5 * wave_step * r[h][c])
            return 0
        lax.fori_loop(0, NA, go, 0)

    def smooth(n, last):
        src, zsrc = f.at[n], zf.at[n]

        def go(x, _):
            for c in range(4):
                halves = [src[x + EX, c, h, ROWS, :] for h in range(2)]
                edge = jnp.where(keep, zsrc[x, c], 0.0)
                for h in range(2):
                    cen = halves[h]
                    nxt, prv = (halves[1], edge) if h == 0 else (edge, halves[0])
                    total = (1.0 - filter_weight * 3.0 * filter_taps[0]) * cen
                    for j in (1, 2, 3):
                        t = ((src[x + EX + j, c, h, ROWS, :] + src[x + EX - j, c, h, ROWS, :])
                             + (src[x + EX, c, h, pl.ds(R0 + j, NY), :] + src[x + EX, c, h, pl.ds(R0 - j, NY), :])
                             + (ahead(cen, nxt, j) + behind(cen, prv, j)))
                        total = total - (filter_weight * filter_taps[j]) * t
                    if last:
                        stage[pl.ds(x * 128 + h * 4 + c, NY, stride=8), :] = total
                    else:
                        f[n + 1, x + EX, c, h, ROWS, :] = total
            return 0
        lax.fori_loop(0, NA, go, 0)

    eddies[0].wait()
    eddy(0)
    eddies[1].start()
    restrict(0)
    eddies[1].wait()
    eddy(1)
    restrict(1)

    halos[0].wait()
    attach(0)
    first(0, 0)
    halos[1].start()
    halos[1].wait()
    second(1, 0)
    halos[2].start()
    halos[2].wait()
    smooth(2, False)
    halos[3].start()
    halos[3].wait()
    attach(1)
    first(3, 1)
    halos[4].start()
    halos[4].wait()
    second(4, 1)
    halos[5].start()
    halos[5].wait()
    smooth(5, True)
    done = pltpu.make_async_copy(stage, out, local.at[0])
    done.start()
    for h in halos + eddies:
        h.drain()
    for a, b in terms:
        pl.when(has_r)(a.wait_send)
        pl.when(has_l)(b.wait_send)
    done.wait()


def solution(mesh):
    count = mesh.shape["gx"]
    placed = (
        P("gx", "gy", None, "grp"),
        P("gx", "gy"),
        P("gx", "gy", None, None, None),
        P("gx"),
        P("gx", "gy", None, "grp"),
    )

    def body(les_velocity, mean_mach, transfer_tiles, intersection_offset, acoustic_state):
        les = les_velocity.transpose(0, 2, 1, 3)
        state = acoustic_state.reshape(NA, NY, 4, 2, L).transpose(0, 1, 3, 2, 4).reshape(NA * NY * 8, L)
        anywhere = pl.BlockSpec(memory_space=pl.ANY)
        result = pl.pallas_call(
            functools.partial(kernel, count),
            out_shape=jax.ShapeDtypeStruct(state.shape, F32),
            in_specs=[anywhere, anywhere, anywhere, pl.BlockSpec(memory_space=pltpu.SMEM), anywhere],
            out_specs=anywhere,
            scratch_shapes=[
                pltpu.VMEM((NX + 2, 3, 2, 32, L), F32),
                pltpu.VMEM((NX + 2, 3, 2, 32, L), F32),
                pltpu.VMEM((2, NX, 3, NY, L), F32),
                pltpu.VMEM((STAGES, NA + 2 * EX, 4, 2, 32, L), F32),
                pltpu.VMEM((STAGES, NA, 4, NY, L), F32),
                pltpu.VMEM((NA * NY * 8, L), F32),
                pltpu.VMEM((8 * 128, 6 * L), BF16),
                pltpu.VMEM((6, 768, 64), BF16),
                pltpu.VMEM((2, NA, 3, 2, NY, L), F32),
                pltpu.VMEM((2, 4, 4, 3, 2, NY, L), F32),
                pltpu.VMEM((NA, NY, L), F32),
                pltpu.VMEM((8, 2, 64, 64), BF16),
                pltpu.VMEM((NA, NY), F32),
                pltpu.SemaphoreType.DMA((4 * (STAGES + 2) + 4,)),
                pltpu.SemaphoreType.DMA((4 * (STAGES + 2) + 4,)),
                pltpu.SemaphoreType.DMA((8,)),
            ],
            compiler_params=pltpu.CompilerParams(collective_id=0, has_side_effects=True, vmem_limit_bytes=60 << 20),
        )(les, mean_mach, transfer_tiles[:, 0], intersection_offset, state)
        return result.reshape(NA, NY, 2, 4, L).transpose(0, 1, 3, 2, 4).reshape(acoustic_state.shape)

    return jax.shard_map(body, mesh=mesh, in_specs=placed, out_specs=P("gx", "gy", None, "grp"), check_vma=False)
```

time: 470 us -> 92.7 us (0.20)
  the two profiles are of different devices: /device:TPU:96 before, /device:TPU:92 now
where the time goes in v1:
time: 92.7 us; the launch traced here: 92.6 us
  Pallas kernels  90.1 us (97%)
  local copies, waits for them, and re-layouts  2.42 us (3%)
    pallas_call x1, Pallas kernels, body(): pl.pallas_call(functools.partial(kernel, count), out_shape=jax.ShapeDtype...  90.1 us
    unnamed x1, local copies, waits for them, and re-layouts  2.42 us

profile of v1, /device:TPU:92, one launch (start us, length us, event | category | flops | bytes accessed | tf_op | source)
XLA Modules:
  0.0 92.6 jit_solution(10862038892670936205)
XLA Ops:
  0.0 90.1 %shard_map.55 = f32[2048,128]{1,0:T(8,128)} custom-call(f32[32,3,16,256]{3,2,1,0:T(8,128)} %bitcast.13, f32[16,16]{1,0:T(8,128)} %mach.1, bf16[8,2,64,64]{3,2,1,0:T(8,128)(2,1)} %bitcast.15, s32[8]{0:T(128)} %offs.1, f32[2048,128]{1,0:T(8,128)} %bitcast.14), custom_call_target="tpu_custom_call" | custom-call | tf_op jit(solution)/shard_map/pallas_call | solution.py:369
  90.2 2.4 %copy.9 = f32[16,16,4,256]{3,2,1,0:T(4,128)} copy(f32[16,16,4,256]{3,2,1,0:T(4,128)} %bitcast.12) | data formatting | bytes 2097152

commit v2 on v1

v2 whole, which is shorter than its diff:
```python
import functools

import jax
import jax.numpy as jnp
from jax import lax
from jax.experimental import pallas as pl
from jax.experimental.pallas import tpu as pltpu
from jax.sharding import PartitionSpec as P

MESH = pl.DeviceIdType.MESH
F32, BF16 = jnp.float32, jnp.bfloat16

eddy_step = 0.1
viscosity = 0.5
wave_step = 0.2
filter_weight = 0.2
derivative_weights = (0.770882380518, -0.166705904415, 0.02084314277)
filter_taps = (0.28739284246, -0.226146951809, 0.10630357877, -0.023853048191)

NX, NA, NY, L = 32, 16, 16, 128
R0 = 8
EX = 3
STAGES = 6
QV, QP, QW, QU = 0, 1, 2, 3
ORDER = (QP, QU, QV, QW)
ROWS = pl.ds(R0, NY)


def kernel(count, les, mach, tiles, offs, state, out, v0, v1, zv, f, zf, stage, lb, wk, s, tb, mb, tl, mc,
           send, recv, local):
    ix, iy, ig = lax.axis_index("gx"), lax.axis_index("gy"), lax.axis_index("grp")
    has_l, has_r = ix > 0, ix < count - 1
    right = {"gx": jnp.minimum(ix + 1, count - 1)}
    left = {"gx": jnp.maximum(ix - 1, 0)}
    side, twin = {"gy": 1 - iy}, {"grp": 1 - ig}

    bar = pltpu.get_barrier_semaphore()

    @pl.when(has_l)
    def _():
        pl.semaphore_signal(bar, inc=1, device_id=left, device_id_type=MESH)

    @pl.when(has_r)
    def _():
        pl.semaphore_signal(bar, inc=1, device_id=right, device_id_type=MESH)

    pl.semaphore_signal(bar, inc=1, device_id=side, device_id_type=MESH)
    pl.semaphore_signal(bar, inc=1, device_id=twin, device_id_type=MESH)

    loads = []
    for h in range(2):
        loads.append(pltpu.make_async_copy(les.at[:, :, :, pl.ds(L * h, L)], v0.at[pl.ds(1, NX), :, h, ROWS, :], local.at[h]))
    loads.append(pltpu.make_async_copy(state, stage, local.at[2]))
    loads.append(pltpu.make_async_copy(tiles, tl, local.at[3]))
    loads.append(pltpu.make_async_copy(mach, mc, local.at[4]))
    for c in loads:
        c.start()

    def clear(ref, width):
        n = ref.shape[0]

        def go(x, _):
            at = pl.multiple_of(jnp.where(iy == 0, 0, 24), 8)
            ref[x, :, :, pl.ds(at, 8), :] = jnp.zeros(ref.shape[1:3] + (8, L), F32)
            return 0
        lax.fori_loop(width, n - width, go, 0)

        @pl.when(jnp.logical_not(has_l))
        def _():
            for x in range(width):
                ref[x, :, :, ROWS, :] = jnp.zeros(ref.shape[1:3] + (NY, L), F32)

        @pl.when(jnp.logical_not(has_r))
        def _():
            for x in range(n - width, n):
                ref[x, :, :, ROWS, :] = jnp.zeros(ref.shape[1:3] + (NY, L), F32)

    def remote(src, dst, to):
        k = remote.count
        remote.count += 1
        return pltpu.make_async_remote_copy(src, dst, send.at[k], recv.at[k], device_id=to, device_id_type=MESH)

    remote.count = 0
    sent = []

    class Sides:
        def __init__(self, pairs):
            self.low, self.high = [remote(*pairs[0], right)], [remote(*pairs[1], left)]
            sent.append(self)

        def start(self):
            pl.when(has_r)(self.low[0].start)
            pl.when(has_l)(self.high[0].start)

        def wait(self):
            pl.when(has_l)(self.low[0].wait_recv)
            pl.when(has_r)(self.high[0].wait_recv)

        def drain(self):
            pl.when(has_r)(self.low[0].wait_send)
            pl.when(has_l)(self.high[0].wait_send)

    class Cross:
        def __init__(self, ref, zref, margin, width, x0, nx, all_fields):
            at, zat = pl.ds(margin + x0, nx), pl.ds(x0, nx)
            fy, fz = (slice(None),) * 2 if all_fields else (pl.ds(QV, 2), pl.ds(QP, 2))
            src = jnp.where(iy == 0, R0 + NY - width, R0)
            dst = jnp.where(iy == 0, R0 - width, R0 + NY)
            self.side = remote(ref.at[at, fy, :, pl.ds(src, width), :], ref.at[at, fy, :, pl.ds(dst, width), :], side)
            self.twin = remote(ref.at[at, fz, 1 - ig, ROWS, :], zref.at[zat, fz], twin)
            sent.append(self)

        def start(self):
            self.side.start()
            self.twin.start()

        def wait(self):
            self.twin.wait_recv()
            self.side.wait_recv()

        def drain(self):
            self.side.wait_send()
            self.twin.wait_send()

    def layers(ref, margin, own, width, fields, h):
        def at(x0):
            return ref.at[pl.ds(margin + x0, width), :, h, ROWS, :] if h is not None else ref.at[pl.ds(margin + x0, width), :, :, ROWS, :]
        return Sides(((at(own - width), at(-width)), (at(0), at(own))))

    veils = [(layers(v, 1, NX, 1, 3, None), Cross(v, zv.at[n], 1, 1, 0, NX, True)) for n, v in enumerate((v0, v1))]
    sides, cross = [], []
    for n in range(STAGES):
        sides.append([layers(f.at[n], EX, NA, EX, 4, h) for h in range(2)] if n else [layers(f.at[n], EX, NA, EX, 4, None)])
        cuts = (((0, NA),), ((4, 8), (0, 4), (12, 4)))[n] if n < 2 else ((3, 10), (0, 3), (13, 3))
        cross.append([Cross(f.at[n], zf.at[n], EX, EX, x0, nx, n in (2, 5)) for x0, nx in cuts])
    terms = [[Sides(((tb.at[n, 3, h], tb.at[n, 0, h]), (tb.at[n, 2, h], tb.at[n, 1, h]))) for h in range(2)] for n in range(2)]

    clear(v0, 1)
    loads[0].wait()
    loads[1].wait()
    pl.semaphore_wait(bar, 2 + has_l.astype(jnp.int32) + has_r.astype(jnp.int32))
    veils[0][0].start()
    veils[0][1].start()

    loads[2].wait()

    def relayout(x, _):
        for h in range(2):
            for c in range(4):
                f[0, x + EX, ORDER[c], h, ROWS, :] = stage[pl.ds(x * 128 + h * 4 + c, NY, stride=8), :]
        return 0

    lax.fori_loop(0, NA, relayout, 0)
    sides[0][0].start()
    cross[0][0].start()

    clear(v1, 1)
    for n in range(STAGES):
        clear(f.at[n], EX)
    for n in range(2):
        @pl.when(jnp.logical_not(has_l))
        def _():
            tb[n, 0] = jnp.zeros(tb.shape[2:], F32)

        @pl.when(jnp.logical_not(has_r))
        def _():
            tb[n, 1] = jnp.zeros(tb.shape[2:], F32)

    loads[3].wait()
    loads[4].wait()

    flow = jnp.transpose(mc[...])
    for x in range(NA):
        mb[x] = jnp.broadcast_to(flow[:, x:x + 1], (NY, L))

    for m in range(-1, 5):
        for j in range(6):
            b = 2 * m - 2 + j
            if not 0 <= b < 8:
                continue
            if j in (2, 3):
                t = tl[b, 0]
            else:
                way = 1.0 if j < 2 else -1.0
                w = 0.5 + 0.5 * way * offs[b].astype(F32)
                t = (tl[b, 1].astype(F32) * w).astype(BF16)
            wk[m + 1, pl.ds(j * 128, 64), :] = t
            wk[m + 1, pl.ds(j * 128 + 64, 64), :] = t

    lane = lax.broadcasted_iota(jnp.int32, (NY, L), 1)
    keep = (lane >= 64).astype(jnp.int32) == ig

    def ahead(cur, nxt, j):
        return pltpu.roll(jnp.where(lane < j, nxt, cur), L - j, 1)

    def behind(cur, prv, j):
        return pltpu.roll(jnp.where(lane >= L - j, prv, cur), j, 1)

    def eddy(n, x):
        src, zsrc = (v0, v1)[n], zv.at[n]
        b, i = x // 4, lax.rem(x, 4)
        halves = [[src[x + 1, c, h, ROWS, :] for h in range(2)] for c in range(3)]
        edge = [jnp.where(keep, zsrc[x, c], 0.0) for c in range(3)]
        for h in range(2):
            grads, laps = [], []
            for c in range(3):
                cen = halves[c][h]
                xp, xm = src[x + 2, c, h, ROWS, :], src[x, c, h, ROWS, :]
                yp, ym = src[x + 1, c, h, pl.ds(R0 + 1, NY), :], src[x + 1, c, h, pl.ds(R0 - 1, NY), :]
                if n == 0 or c < 2:
                    nxt, prv = (halves[c][1], edge[c]) if h == 0 else (edge[c], halves[c][0])
                    zp, zm = ahead(cen, nxt, 1), behind(cen, prv, 1)
                else:
                    zp = zm = cen
                grads.append((0.5 * (xp - xm), 0.5 * (yp - ym), 0.5 * (zp - zm)))
                if n == 0:
                    laps.append(((xp + xm) + (yp + ym)) + ((zp + zm) - 6.0 * cen))
            u, v, w = (halves[c][h] for c in range(3))
            ox = grads[2][1] - grads[1][2]
            oy = grads[0][2] - grads[2][0]
            oz = grads[1][0] - grads[0][1]
            lamb = (oy * w - oz * v, oz * u - ox * w, ox * v - oy * u)
            for c in range(3):
                hi = lamb[c].astype(BF16)
                lo = (lamb[c] - hi.astype(F32)).astype(BF16)
                at = pl.multiple_of(b * 128 + i * 16, 16)
                lb[pl.ds(at, 16), pl.ds((h * 3 + c) * L, L)] = hi
                lb[pl.ds(at + 64, 16), pl.ds((h * 3 + c) * L, L)] = lo
                if n == 0:
                    v1[x + 1, c, h, ROWS, :] = halves[c][h] + eddy_step * (viscosity * laps[c] - lamb[c])

    def product(m, h=None):
        j0, j1 = max(0, 2 - 2 * m), min(6, 10 - 2 * m)
        rows = pl.ds((2 * m - 2 + j0) * 128, (j1 - j0) * 128)
        cols = pl.ds(0, 6 * L) if h is None else pl.ds(h * 3 * L, 3 * L)
        return lax.dot_general(wk[m + 1, pl.ds(j0 * 128, (j1 - j0) * 128), :], lb[rows, cols],
                               (((0,), (0,)), ((), ())), preferred_element_type=F32)

    def rim_terms(n, h):
        for m, slot in ((4, 3), (-1, 2)):
            r = product(m, h)
            for i in range(4):
                for c in range(3):
                    tb[n, slot, h, i, c] = r[i * 16:(i + 1) * 16, c * L:(c + 1) * L]

    def own_terms(n):
        for m in range(4):
            r = product(m)
            for i in range(4):
                for c in range(3):
                    for h in range(2):
                        s[n, 4 * m + i, c, h] = r[i * 16:(i + 1) * 16, (h * 3 + c) * L:(h * 3 + c + 1) * L]

    def attach(n, h):
        for i in range(4):
            for c in range(3):
                s[n, i, c, h] = s[n, i, c, h] + tb[n, 0, h, i, c]
                s[n, 12 + i, c, h] = s[n, 12 + i, c, h] + tb[n, 1, h, i, c]

    def slope(ahead_, behind_):
        total = None
        for j in range(3):
            t = derivative_weights[j] * (ahead_[j] - behind_[j])
            total = t if total is None else total + t
        return total

    def beside(n, x, c, h):
        edge = jnp.where(keep, zf[n, x, c], 0.0)
        other = f[n, x + EX, c, 1 - h, ROWS, :]
        return (other, edge) if h == 0 else (edge, other)

    def rate(n, k, x, h):
        src = f.at[n]
        cen = [src[x + EX, c, h, ROWS, :] for c in range(4)]
        m = mb[x]

        def dx(c):
            return slope([src[x + EX + j, c, h, ROWS, :] for j in (1, 2, 3)], [src[x + EX - j, c, h, ROWS, :] for j in (1, 2, 3)])

        def dy(c):
            return slope([src[x + EX, c, h, pl.ds(R0 + j, NY), :] for j in (1, 2, 3)],
                         [src[x + EX, c, h, pl.ds(R0 - j, NY), :] for j in (1, 2, 3)])

        def dz(c):
            nxt, prv = beside(n, x, c, h)
            return slope([ahead(cen[c], nxt, j) for j in (1, 2, 3)], [behind(cen[c], prv, j) for j in (1, 2, 3)])

        d = [dx(c) for c in range(4)]
        r = [None] * 4
        r[QP] = -(m * d[QP] + d[QU] + dy(QV) + dz(QW))
        r[QU] = -(m * d[QU] + d[QP]) - s[k, x, 0, h]
        r[QV] = -(m * d[QV] + dy(QP)) - s[k, x, 1, h]
        r[QW] = -(m * d[QW] + dz(QP)) - s[k, x, 2, h]
        return cen, r

    def first(n, k, x, h):
        cen, r = rate(n, k, x, h)
        for c in range(4):
            f[n + 1, x + EX, c, h, ROWS, :] = cen[c] + wave_step * r[c]

    def second(n, k, x, h):
        cen, r = rate(n, k, x, h)
        for c in range(4):
            f[n + 1, x + EX, c, h, ROWS, :] = 0.5 * (f[n - 1, x + EX, c, h, ROWS, :] + cen[c]) + 0.5 * wave_step * r[c]

    def smooth(n, x, h):
        src = f.at[n]
        for q, c in enumerate(ORDER):
            cen = src[x + EX, c, h, ROWS, :]
            nxt, prv = beside(n, x, c, h)
            total = (1.0 - filter_weight * 3.0 * filter_taps[0]) * cen
            for j in (1, 2, 3):
                t = ((src[x + EX + j, c, h, ROWS, :] + src[x + EX - j, c, h, ROWS, :])
                     + (src[x + EX, c, h, pl.ds(R0 + j, NY), :] + src[x + EX, c, h, pl.ds(R0 - j, NY), :])
                     + (ahead(cen, nxt, j) + behind(cen, prv, j)))
                total = total - (filter_weight * filter_taps[j]) * t
            if n + 1 == STAGES:
                stage[pl.ds(x * 128 + h * 4 + q, NY, stride=8), :] = total
            else:
                f[n + 1, x + EX, c, h, ROWS, :] = total

    def over(lo, hi, step):
        def go(x, _):
            step(x)
            return 0
        lax.fori_loop(lo, hi, go, 0)

    def both(step):
        def go(x):
            step(x, 0)
            step(x, 1)
        return go

    def rim(width, step):
        def go(i):
            step(jnp.where(i < width, i, i + NA - 2 * width))
        over(0, 2 * width, go)

    veils[0][1].wait()
    over(1, NX - 1, functools.partial(eddy, 0))
    veils[0][0].wait()
    over(0, 2, lambda i: eddy(0, i * (NX - 1)))
    for h in range(2):
        rim_terms(0, h)
        terms[0][h].start()
    for c in veils[1]:
        c.start()
    own_terms(0)

    cross[0][0].wait()
    sides[0][0].wait()
    over(0, NA, both(functools.partial(first, 0, 0)))
    cross[1][0].start()
    for h in range(2):
        terms[0][h].wait()

        def mend(i):
            for c, q in enumerate((QU, QV, QW)):
                for x0, slot in ((0, 0), (12, 1)):
                    old = f[1, x0 + i + EX, q, h, ROWS, :]
                    f[1, x0 + i + EX, q, h, ROWS, :] = old - wave_step * tb[0, slot, h, i, c]
        over(0, 4, mend)
        sides[1][h].start()
    cross[1][1].start()
    cross[1][2].start()
    for h in range(2):
        attach(0, h)

    for n in range(1, STAGES):
        step = (functools.partial(first, n, n // 3), functools.partial(second, n, n // 3), functools.partial(smooth, n))[n % 3]
        cross[n][0].wait()
        if n == 1:
            cross[n][1].wait()
            cross[n][2].wait()
        over(3, 13, both(step))
        if n + 1 < STAGES:
            cross[n + 1][0].start()
        else:
            inner = pltpu.make_async_copy(stage.at[pl.ds(3 * 128, 10 * 128)], out.at[pl.ds(3 * 128, 10 * 128)], local.at[0])
            inner.start()
        if n == 1:
            for c in veils[1]:
                c.wait()
            over(0, NX, functools.partial(eddy, 1))
            for h in range(2):
                rim_terms(1, h)
            own_terms(1)
        if n == 2:
            for h in range(2):
                terms[1][h].wait()
                attach(1, h)
        if n > 1:
            cross[n][1].wait()
            cross[n][2].wait()
        for h in range(2):
            sides[n][h].wait()
            rim(EX, lambda x: step(x, h))
            if n + 1 < STAGES:
                sides[n + 1][h].start()
        if n + 1 < STAGES:
            cross[n + 1][1].start()
            cross[n + 1][2].start()
        if n == 1:
            for h in range(2):
                terms[1][h].start()
    outer = [pltpu.make_async_copy(stage.at[pl.ds(x * 128, 3 * 128)], out.at[pl.ds(x * 128, 3 * 128)], local.at[k])
             for k, x in ((1, 0), (2, 13))]
    for c in outer:
        c.start()
    for c in sent:
        c.drain()
    inner.wait()
    for c in outer:
        c.wait()


def solution(mesh):
    count = mesh.shape["gx"]
    placed = (
        P("gx", "gy", None, "grp"),
        P("gx", "gy"),
        P("gx", "gy", None, None, None),
        P("gx"),
        P("gx", "gy", None, "grp"),
    )

    def body(les_velocity, mean_mach, transfer_tiles, intersection_offset, acoustic_state):
        les = les_velocity.transpose(0, 2, 1, 3)
        state = acoustic_state.reshape(NA, NY, 4, 2, L).transpose(0, 1, 3, 2, 4).reshape(NA * NY * 8, L)
        anywhere = pl.BlockSpec(memory_space=pl.ANY)
        result = pl.pallas_call(
            functools.partial(kernel, count),
            out_shape=jax.ShapeDtypeStruct(state.shape, F32),
            in_specs=[anywhere, anywhere, anywhere, pl.BlockSpec(memory_space=pltpu.SMEM), anywhere],
            out_specs=anywhere,
            scratch_shapes=[
                pltpu.VMEM((NX + 2, 3, 2, 32, L), F32),
                pltpu.VMEM((NX + 2, 3, 2, 32, L), F32),
                pltpu.VMEM((2, NX, 3, NY, L), F32),
                pltpu.VMEM((STAGES, NA + 2 * EX, 4, 2, 32, L), F32),
                pltpu.VMEM((STAGES, NA, 4, NY, L), F32),
                pltpu.VMEM((NA * NY * 8, L), F32),
                pltpu.VMEM((8 * 128, 6 * L), BF16),
                pltpu.VMEM((6, 768, 64), BF16),
                pltpu.VMEM((2, NA, 3, 2, NY, L), F32),
                pltpu.VMEM((2, 4, 2, 4, 3, NY, L), F32),
                pltpu.VMEM((NA, NY, L), F32),
                pltpu.VMEM((8, 2, 64, 64), BF16),
                pltpu.VMEM((NA, NY), F32),
                pltpu.SemaphoreType.DMA((72,)),
                pltpu.SemaphoreType.DMA((72,)),
                pltpu.SemaphoreType.DMA((8,)),
            ],
            compiler_params=pltpu.CompilerParams(collective_id=0, has_side_effects=True, vmem_limit_bytes=60 << 20),
        )(les, mean_mach, transfer_tiles[:, 0], intersection_offset, state)
        return result.reshape(NA, NY, 2, 4, L).transpose(0, 1, 3, 2, 4).reshape(acoustic_state.shape)

    return jax.shard_map(body, mesh=mesh, in_specs=placed, out_specs=P("gx", "gy", None, "grp"), check_vma=False)
```

time: 92.7 us -> 75.5 us (0.81)
  the two profiles are of different devices: /device:TPU:92 before, /device:TPU:1 now
where the time goes in v2:
time: 75.5 us; the launch traced here: 74.2 us
  Pallas kernels  71.8 us (95%)
  local copies, waits for them, and re-layouts  2.42 us (3%)
    pallas_call x1, Pallas kernels, body(): pl.pallas_call(functools.partial(kernel, count), out_shape=jax.ShapeDtype...  71.8 us
    unnamed x1, local copies, waits for them, and re-layouts  2.42 us

profile of v2, /device:TPU:1, one launch (start us, length us, event | category | flops | bytes accessed | tf_op | source)
XLA Modules:
  0.0 74.2 jit_solution(2542449776602015779)
XLA Ops:
  0.0 71.8 %shard_map.55 = f32[2048,128]{1,0:T(8,128)} custom-call(f32[32,3,16,256]{3,2,1,0:T(8,128)} %bitcast.13, f32[16,16]{1,0:T(8,128)} %mach.1, bf16[8,2,64,64]{3,2,1,0:T(8,128)(2,1)} %bitcast.15, s32[8]{0:T(128)} %offs.1, f32[2048,128]{1,0:T(8,128)} %bitcast.14), custom_call_target="tpu_custom_call" | custom-call | tf_op jit(solution)/shard_map/pallas_call | solution.py:431
  71.8 2.4 %copy.9 = f32[16,16,4,256]{3,2,1,0:T(4,128)} copy(f32[16,16,4,256]{3,2,1,0:T(4,128)} %bitcast.12) | data formatting | bytes 2097152

commit v3 on v2

--- a/solution.py
+++ b/solution.py
@@ -26,13 +26,17 @@
 ROWS = pl.ds(R0, NY)
 
 
-def kernel(count, les, mach, tiles, offs, state, out, v0, v1, zv, f, zf, stage, lb, wk, s, tb, mb, tl, mc,
-           send, recv, local):
+def kernel(count, les, mach, tiles, offs, state, out, *refs):
+    (v0, v1, *zv), refs = refs[:4], refs[4:]
+    f, zf, xh, yh, refs = *(refs[k * STAGES:(k + 1) * STAGES] for k in range(4)), refs[4 * STAGES:]
+    s, tb, (stage, lb, wk, mb, tl, mc, send, recv, local) = refs[:2], refs[2:4], refs[4:]
     ix, iy, ig = lax.axis_index("gx"), lax.axis_index("gy"), lax.axis_index("grp")
     has_l, has_r = ix > 0, ix < count - 1
     right = {"gx": jnp.minimum(ix + 1, count - 1)}
     left = {"gx": jnp.maximum(ix - 1, 0)}
     side, twin = {"gy": 1 - iy}, {"grp": 1 - ig}
+    later = ((ix == count // 2 - 1) | (ix == count // 2)) & (iy == 1)
+    sooner = jnp.logical_not(later)
 
     bar = pltpu.get_barrier_semaphore()
 
@@ -56,24 +60,36 @@
     for c in loads:
         c.start()
 
-    def clear(ref, width):
+    def clear(ref, width, always):
         n = ref.shape[0]
 
         def go(x, _):
-            at = pl.multiple_of(jnp.where(iy == 0, 0, 24), 8)
+            if always:
+                for at in (0, 24):
+                    ref[x, :, :, pl.ds(at, 8), :] = jnp.zeros(ref.shape[1:3] + (8, L), F32)
+            else:
+                at = pl.multiple_of(jnp.where(iy == 0, 0, 24), 8)
+                ref[x, :, :, pl.ds(at, 8), :] = jnp.zeros(ref.shape[1:3] + (8, L), F32)
+            return 0
+        lax.fori_loop(width, n - width, go, 0)
+
+        def ends(low):
+            for x in range(width):
+                ref[x if low else n - 1 - x, :, :, ROWS, :] = jnp.zeros(ref.shape[1:3] + (NY, L), F32)
+
+        if always:
+            ends(True)
+            ends(False)
+        else:
+            pl.when(jnp.logical_not(has_l))(lambda: ends(True))
+            pl.when(jnp.logical_not(has_r))(lambda: ends(False))
+
+    def clear_rows(ref):
+        def go(x, _):
+            at = pl.multiple_of(8 * iy, 8)
             ref[x, :, :, pl.ds(at, 8), :] = jnp.zeros(ref.shape[1:3] + (8, L), F32)
             return 0
-        lax.fori_loop(width, n - width, go, 0)
-
-        @pl.when(jnp.logical_not(has_l))
-        def _():
-            for x in range(width):
-                ref[x, :, :, ROWS, :] = jnp.zeros(ref.shape[1:3] + (NY, L), F32)
-
-        @pl.when(jnp.logical_not(has_r))
-        def _():
-            for x in range(n - width, n):
-                ref[x, :, :, ROWS, :] = jnp.zeros(ref.shape[1:3] + (NY, L), F32)
+        lax.fori_loop(0, NA, go, 0)
 
     def remote(src, dst, to):
         k = remote.count
@@ -101,12 +117,17 @@
             pl.when(has_l)(self.high[0].wait_send)
 
     class Cross:
-        def __init__(self, ref, zref, margin, width, x0, nx, all_fields):
+        def __init__(self, ref, yref, zref, margin, width, x0, nx, all_fields):
             at, zat = pl.ds(margin + x0, nx), pl.ds(x0, nx)
             fy, fz = (slice(None),) * 2 if all_fields else (pl.ds(QV, 2), pl.ds(QP, 2))
             src = jnp.where(iy == 0, R0 + NY - width, R0)
             dst = jnp.where(iy == 0, R0 - width, R0 + NY)
-            self.side = remote(ref.at[at, fy, :, pl.ds(src, width), :], ref.at[at, fy, :, pl.ds(dst, width), :], side)
+            self.heard = False
+            if yref is None:
+                target = ref.at[at, fy, :, pl.ds(dst, width), :]
+            else:
+                target = yref.at[zat, fy, :, pl.ds(jnp.where(iy == 0, 8 - width, 8), width), :]
+            self.side = remote(ref.at[at, fy, :, pl.ds(src, width), :], target, side)
             self.twin = remote(ref.at[at, fz, 1 - ig, ROWS, :], zref.at[zat, fz], twin)
             sent.append(self)
 
@@ -115,27 +136,44 @@
             self.twin.start()
 
         def wait(self):
+            self.wait_twin()
+            self.wait_side()
+
+        def wait_twin(self):
             self.twin.wait_recv()
+
+        def wait_side(self):
+            if self.heard:
+                pl.when(sooner)(self.side.wait_recv)
+            else:
+                self.side.wait_recv()
+
+        def hear(self):
+            self.heard = True
             self.side.wait_recv()
 
         def drain(self):
             self.side.wait_send()
             self.twin.wait_send()
 
-    def layers(ref, margin, own, width, fields, h):
-        def at(x0):
-            return ref.at[pl.ds(margin + x0, width), :, h, ROWS, :] if h is not None else ref.at[pl.ds(margin + x0, width), :, :, ROWS, :]
-        return Sides(((at(own - width), at(-width)), (at(0), at(own))))
-
-    veils = [(layers(v, 1, NX, 1, 3, None), Cross(v, zv.at[n], 1, 1, 0, NX, True)) for n, v in enumerate((v0, v1))]
+    def rims(n, h):
+        half = slice(None) if h is None else h
+        return Sides(((f[n].at[pl.ds(EX + NA - EX, EX), :, half, ROWS, :], xh[n].at[0, :, :, half]),
+                      (f[n].at[pl.ds(EX, EX), :, half, ROWS, :], xh[n].at[1, :, :, half])))
+
+    def veil(v):
+        return Sides(((v.at[pl.ds(NX, 1), :, :, ROWS, :], v.at[pl.ds(0, 1), :, :, ROWS, :]),
+                      (v.at[pl.ds(1, 1), :, :, ROWS, :], v.at[pl.ds(NX + 1, 1), :, :, ROWS, :])))
+
+    veils = [(veil(v), Cross(v, None, zv[n], 1, 1, 0, NX, True)) for n, v in enumerate((v0, v1))]
     sides, cross = [], []
     for n in range(STAGES):
-        sides.append([layers(f.at[n], EX, NA, EX, 4, h) for h in range(2)] if n else [layers(f.at[n], EX, NA, EX, 4, None)])
-        cuts = (((0, NA),), ((4, 8), (0, 4), (12, 4)))[n] if n < 2 else ((3, 10), (0, 3), (13, 3))
-        cross.append([Cross(f.at[n], zf.at[n], EX, EX, x0, nx, n in (2, 5)) for x0, nx in cuts])
-    terms = [[Sides(((tb.at[n, 3, h], tb.at[n, 0, h]), (tb.at[n, 2, h], tb.at[n, 1, h]))) for h in range(2)] for n in range(2)]
-
-    clear(v0, 1)
+        sides.append([rims(n, h) for h in range(2)])
+        cuts = ((0, NA),) if n == 0 else ((4, 8), (0, 4), (12, 4)) if n % 3 == 1 else ((3, 10), (0, 3), (13, 3))
+        cross.append([Cross(f[n], yh[n], zf[n], EX, EX, x0, nx, n in (2, 5)) for x0, nx in cuts])
+    terms = [[Sides(((tb[n].at[3, h], tb[n].at[0, h]), (tb[n].at[2, h], tb[n].at[1, h]))) for h in range(2)] for n in range(2)]
+
+    clear(v0, 1, False)
     loads[0].wait()
     loads[1].wait()
     pl.semaphore_wait(bar, 2 + has_l.astype(jnp.int32) + has_r.astype(jnp.int32))
@@ -147,24 +185,28 @@
     def relayout(x, _):
         for h in range(2):
             for c in range(4):
-                f[0, x + EX, ORDER[c], h, ROWS, :] = stage[pl.ds(x * 128 + h * 4 + c, NY, stride=8), :]
+                f[0][x + EX, ORDER[c], h, ROWS, :] = stage[pl.ds(x * 128 + h * 4 + c, NY, stride=8), :]
         return 0
 
     lax.fori_loop(0, NA, relayout, 0)
-    sides[0][0].start()
+    for h in range(2):
+        sides[0][h].start()
     cross[0][0].start()
-
-    clear(v1, 1)
-    for n in range(STAGES):
-        clear(f.at[n], EX)
+    clear(f[0], EX, True)
+    clear_rows(yh[0])
+
+    clear(v1, 1, False)
+    for n in range(1, STAGES):
+        clear(f[n], EX, True)
+        clear_rows(yh[n])
     for n in range(2):
         @pl.when(jnp.logical_not(has_l))
         def _():
-            tb[n, 0] = jnp.zeros(tb.shape[2:], F32)
+            tb[n][0] = jnp.zeros(tb[n].shape[1:], F32)
 
         @pl.when(jnp.logical_not(has_r))
         def _():
-            tb[n, 1] = jnp.zeros(tb.shape[2:], F32)
+            tb[n][1] = jnp.zeros(tb[n].shape[1:], F32)
 
     loads[3].wait()
     loads[4].wait()
@@ -197,7 +239,7 @@
         return pltpu.roll(jnp.where(lane >= L - j, prv, cur), j, 1)
 
     def eddy(n, x):
-        src, zsrc = (v0, v1)[n], zv.at[n]
+        src, zsrc = (v0, v1)[n], zv[n]
         b, i = x // 4, lax.rem(x, 4)
         halves = [[src[x + 1, c, h, ROWS, :] for h in range(2)] for c in range(3)]
         edge = [jnp.where(keep, zsrc[x, c], 0.0) for c in range(3)]
@@ -241,7 +283,7 @@
             r = product(m, h)
             for i in range(4):
                 for c in range(3):
-                    tb[n, slot, h, i, c] = r[i * 16:(i + 1) * 16, c * L:(c + 1) * L]
+                    tb[n][slot, h, i, c] = r[i * 16:(i + 1) * 16, c * L:(c + 1) * L]
 
     def own_terms(n):
         for m in range(4):
@@ -249,13 +291,13 @@
             for i in range(4):
                 for c in range(3):
                     for h in range(2):
-                        s[n, 4 * m + i, c, h] = r[i * 16:(i + 1) * 16, (h * 3 + c) * L:(h * 3 + c + 1) * L]
+                        s[n][4 * m + i, c, h] = r[i * 16:(i + 1) * 16, (h * 3 + c) * L:(h * 3 + c + 1) * L]
 
     def attach(n, h):
         for i in range(4):
             for c in range(3):
-                s[n, i, c, h] = s[n, i, c, h] + tb[n, 0, h, i, c]
-                s[n, 12 + i, c, h] = s[n, 12 + i, c, h] + tb[n, 1, h, i, c]
+                s[n][i, c, h] = s[n][i, c, h] + tb[n][0, h, i, c]
+                s[n][12 + i, c, h] = s[n][12 + i, c, h] + tb[n][1, h, i, c]
 
     def slope(ahead_, behind_):
         total = None
@@ -265,12 +307,12 @@
         return total
 
     def beside(n, x, c, h):
-        edge = jnp.where(keep, zf[n, x, c], 0.0)
-        other = f[n, x + EX, c, 1 - h, ROWS, :]
+        edge = jnp.where(keep, zf[n][x, c], 0.0)
+        other = f[n][x + EX, c, 1 - h, ROWS, :]
         return (other, edge) if h == 0 else (edge, other)
 
     def rate(n, k, x, h):
-        src = f.at[n]
+        src = f[n]
         cen = [src[x + EX, c, h, ROWS, :] for c in range(4)]
         m = mb[x]
 
@@ -288,23 +330,23 @@
         d = [dx(c) for c in range(4)]
         r = [None] * 4
         r[QP] = -(m * d[QP] + d[QU] + dy(QV) + dz(QW))
-        r[QU] = -(m * d[QU] + d[QP]) - s[k, x, 0, h]
-        r[QV] = -(m * d[QV] + dy(QP)) - s[k, x, 1, h]
-        r[QW] = -(m * d[QW] + dz(QP)) - s[k, x, 2, h]
+        r[QU] = -(m * d[QU] + d[QP]) - s[k][x, 0, h]
+        r[QV] = -(m * d[QV] + dy(QP)) - s[k][x, 1, h]
+        r[QW] = -(m * d[QW] + dz(QP)) - s[k][x, 2, h]
         return cen, r
 
     def first(n, k, x, h):
         cen, r = rate(n, k, x, h)
         for c in range(4):
-            f[n + 1, x + EX, c, h, ROWS, :] = cen[c] + wave_step * r[c]
+            f[n + 1][x + EX, c, h, ROWS, :] = cen[c] + wave_step * r[c]
 
     def second(n, k, x, h):
         cen, r = rate(n, k, x, h)
         for c in range(4):
-            f[n + 1, x + EX, c, h, ROWS, :] = 0.5 * (f[n - 1, x + EX, c, h, ROWS, :] + cen[c]) + 0.5 * wave_step * r[c]
+            f[n + 1][x + EX, c, h, ROWS, :] = 0.5 * (f[n - 1][x + EX, c, h, ROWS, :] + cen[c]) + 0.5 * wave_step * r[c]
 
     def smooth(n, x, h):
-        src = f.at[n]
+        src = f[n]
         for q, c in enumerate(ORDER):
             cen = src[x + EX, c, h, ROWS, :]
             nxt, prv = beside(n, x, c, h)
@@ -317,13 +359,73 @@
             if n + 1 == STAGES:
                 stage[pl.ds(x * 128 + h * 4 + q, NY, stride=8), :] = total
             else:
-                f[n + 1, x + EX, c, h, ROWS, :] = total
+                f[n + 1][x + EX, c, h, ROWS, :] = total
+
+    def correct_rows(n, x):
+        kind = n % 3
+        taps = [filter_weight * w for w in filter_taps[1:]] if kind == 2 else derivative_weights
+        w = wave_step if kind == 0 else 0.5 * wave_step
+
+        def side_of(low):
+            own = 0 if low else 8
+            for h in range(2):
+                for c in range(4) if kind == 2 else (QV, QP):
+                    total = None
+                    for j in (1, 2, 3):
+                        p = taps[j - 1] * yh[n][x, c, h, pl.ds(8 - j if low else j, 8), :]
+                        total = p if total is None else total + p
+                    to = c if kind == 2 else QP + QV - c
+                    if n + 1 == STAGES:
+                        at = pl.ds(x * 128 + own * 8 + h * 4 + ORDER.index(c), 8, stride=8)
+                        stage[at, :] = stage[at, :] - total
+                    else:
+                        at = pl.ds(R0 + own, 8)
+                        change = total if kind == 2 else (-w if low else w) * total
+                        f[n + 1][x + EX, to, h, at, :] = f[n + 1][x + EX, to, h, at, :] - change
+
+        pl.when(iy == 1)(lambda: side_of(True))
+        pl.when(iy == 0)(lambda: side_of(False))
+
+    def correct(n, h):
+        kind = n % 3
+        taps = [filter_weight * w for w in filter_taps[1:]] if kind == 2 else derivative_weights
+
+        def side_of(low):
+            halo = [[xh[n][0 if low else 1, EX - k if low else k - 1, c, h] for c in range(4)] for k in (1, 2, 3)]
+            for i in range(EX):
+                x = i if low else NA - 1 - i
+                d = []
+                for c in range(4):
+                    total = taps[i] * halo[0][c]
+                    for k in range(1, EX - i):
+                        total = total + taps[i + k] * halo[k][c]
+                    d.append(total)
+                if kind == 2:
+                    change = d
+                else:
+                    w = (wave_step if kind == 0 else 0.5 * wave_step) * (-1.0 if low else 1.0)
+                    m = w * mb[x]
+                    change = [None] * 4
+                    change[QP] = m * d[QP] + w * d[QU]
+                    change[QU] = m * d[QU] + w * d[QP]
+                    change[QV] = m * d[QV]
+                    change[QW] = m * d[QW]
+                for q, c in enumerate(ORDER):
+                    if n + 1 == STAGES:
+                        at = pl.ds(x * 128 + h * 4 + q, NY, stride=8)
+                        stage[at, :] = stage[at, :] - change[c]
+                    else:
+                        f[n + 1][x + EX, c, h, ROWS, :] = f[n + 1][x + EX, c, h, ROWS, :] - change[c]
+
+        pl.when(has_l)(lambda: side_of(True))
+        pl.when(has_r)(lambda: side_of(False))
 
     def over(lo, hi, step):
         def go(x, _):
-            step(x)
+            step(lo + 2 * x)
+            step(lo + 2 * x + 1)
             return 0
-        lax.fori_loop(lo, hi, go, 0)
+        lax.fori_loop(0, (hi - lo) // 2, go, 0)
 
     def both(step):
         def go(x):
@@ -335,6 +437,32 @@
         def go(i):
             step(jnp.where(i < width, i, i + NA - 2 * width))
         over(0, 2 * width, go)
+
+    def mend(k):
+        n = 3 * k + 1
+        for h in range(2):
+            sides[n][h].drain()
+            sent.remove(sides[n][h])
+            terms[k][h].wait()
+
+            def go(i):
+                for c, q in enumerate((QU, QV, QW)):
+                    for x0, slot in ((0, 0), (12, 1)):
+                        f[n][x0 + i + EX, q, h, ROWS, :] = f[n][x0 + i + EX, q, h, ROWS, :] - wave_step * tb[k][slot, h, i, c]
+            over(0, 4, go)
+        cross[n][1].start()
+        cross[n][2].start()
+        for h in range(2):
+            attach(k, h)
+
+    def mend_halo(k, h):
+        n = 3 * k + 1
+        for low, slot, first_layer in ((0, 2, 1), (1, 3, 0)):
+            def go():
+                for j in range(EX):
+                    for c, q in enumerate((QU, QV, QW)):
+                        xh[n][low, j, q, h] = xh[n][low, j, q, h] - wave_step * tb[k][slot, h, j + first_layer, c]
+            pl.when(has_r if low else has_l)(go)
 
     veils[0][1].wait()
     over(1, NX - 1, functools.partial(eddy, 0))
@@ -343,66 +471,60 @@
     for h in range(2):
         rim_terms(0, h)
         terms[0][h].start()
-    for c in veils[1]:
-        c.start()
     own_terms(0)
 
-    cross[0][0].wait()
-    sides[0][0].wait()
-    over(0, NA, both(functools.partial(first, 0, 0)))
-    cross[1][0].start()
-    for h in range(2):
-        terms[0][h].wait()
-
-        def mend(i):
-            for c, q in enumerate((QU, QV, QW)):
-                for x0, slot in ((0, 0), (12, 1)):
-                    old = f[1, x0 + i + EX, q, h, ROWS, :]
-                    f[1, x0 + i + EX, q, h, ROWS, :] = old - wave_step * tb[0, slot, h, i, c]
-        over(0, 4, mend)
-        sides[1][h].start()
-    cross[1][1].start()
-    cross[1][2].start()
-    for h in range(2):
-        attach(0, h)
-
-    for n in range(1, STAGES):
+    for n in range(STAGES):
         step = (functools.partial(first, n, n // 3), functools.partial(second, n, n // 3), functools.partial(smooth, n))[n % 3]
-        cross[n][0].wait()
-        if n == 1:
-            cross[n][1].wait()
-            cross[n][2].wait()
-        over(3, 13, both(step))
-        if n + 1 < STAGES:
-            cross[n + 1][0].start()
-        else:
-            inner = pltpu.make_async_copy(stage.at[pl.ds(3 * 128, 10 * 128)], out.at[pl.ds(3 * 128, 10 * 128)], local.at[0])
-            inner.start()
-        if n == 1:
+        if n == 2:
             for c in veils[1]:
                 c.wait()
             over(0, NX, functools.partial(eddy, 1))
-            for h in range(2):
-                rim_terms(1, h)
+            rim_terms(1, 0)
+            terms[1][0].start()
+            rim_terms(1, 1)
             own_terms(1)
-        if n == 2:
-            for h in range(2):
-                terms[1][h].wait()
-                attach(1, h)
-        if n > 1:
-            cross[n][1].wait()
-            cross[n][2].wait()
+        cross[n][0].wait_twin()
+        if n == 0:
+            over(0, NA, both(step))
+        else:
+            width = 4 if n % 3 == 1 else EX
+            over(width, NA - width, both(step))
+            cross[n][1].wait_twin()
+            cross[n][2].wait_twin()
+            rim(width, lambda x: both(step)(x))
+        for c in cross[n]:
+            c.wait_side()
+        over(0, NA, functools.partial(correct_rows, n))
+        if n + 1 == STAGES:
+            inner = pltpu.make_async_copy(stage.at[pl.ds(3 * 128, 10 * 128)], out.at[pl.ds(3 * 128, 10 * 128)], local.at[0])
+            inner.start()
+        elif n % 3:
+            cross[n + 1][0].start()
         for h in range(2):
             sides[n][h].wait()
-            rim(EX, lambda x: step(x, h))
+            if n % 3 == 1:
+                mend_halo(n // 3, h)
+            correct(n, h)
             if n + 1 < STAGES:
-                sides[n + 1][h].start()
-        if n + 1 < STAGES:
+                pl.when(sooner)(sides[n + 1][h].start)
+        if n % 3 == 0:
+            cross[n + 1][0].start()
+        elif n + 1 < STAGES:
             cross[n + 1][1].start()
             cross[n + 1][2].start()
-        if n == 1:
-            for h in range(2):
-                terms[1][h].start()
+        if n + 1 < STAGES:
+            @pl.when(later)
+            def _():
+                cross[n + 1][0 if n % 3 == 0 else 2].hear()
+                for h in range(2):
+                    sides[n + 1][h].start()
+        if n % 3 == 0:
+            mend(n // 3)
+        if n == 0:
+            for c in veils[1]:
+                c.start()
+        if n == 2:
+            terms[1][1].start()
     outer = [pltpu.make_async_copy(stage.at[pl.ds(x * 128, 3 * 128)], out.at[pl.ds(x * 128, 3 * 128)], local.at[k])
              for k, x in ((1, 0), (2, 13))]
     for c in outer:
@@ -436,14 +558,17 @@
             scratch_shapes=[
                 pltpu.VMEM((NX + 2, 3, 2, 32, L), F32),
                 pltpu.VMEM((NX + 2, 3, 2, 32, L), F32),
-                pltpu.VMEM((2, NX, 3, NY, L), F32),
-                pltpu.VMEM((STAGES, NA + 2 * EX, 4, 2, 32, L), F32),
-                pltpu.VMEM((STAGES, NA, 4, NY, L), F32),
+                pltpu.VMEM((NX, 3, NY, L), F32),
+                pltpu.VMEM((NX, 3, NY, L), F32),
+                *[pltpu.VMEM((NA + 2 * EX, 4, 2, 32, L), F32)] * STAGES,
+                *[pltpu.VMEM((NA, 4, NY, L), F32)] * STAGES,
+                *[pltpu.VMEM((2, EX, 4, 2, NY, L), F32)] * STAGES,
+                *[pltpu.VMEM((NA, 4, 2, NY, L), F32)] * STAGES,
+                *[pltpu.VMEM((NA, 3, 2, NY, L), F32)] * 2,
+                *[pltpu.VMEM((4, 2, 4, 3, NY, L), F32)] * 2,
                 pltpu.VMEM((NA * NY * 8, L), F32),
                 pltpu.VMEM((8 * 128, 6 * L), BF16),
                 pltpu.VMEM((6, 768, 64), BF16),
-                pltpu.VMEM((2, NA, 3, 2, NY, L), F32),
-                pltpu.VMEM((2, 4, 2, 4, 3, NY, L), F32),
                 pltpu.VMEM((NA, NY, L), F32),
                 pltpu.VMEM((8, 2, 64, 64), BF16),
                 pltpu.VMEM((NA, NY), F32),

time: 75.5 us -> 77 us (1.020); the launches traced: 74.2 us -> 76.9 us
  Pallas kernels: 71.8 us -> 74.4 us
    pallas_call x1, Pallas kernels: 71.8 us -> 74.4 us  [body(): pl.pallas_call(functools.partial(kernel, count), out_shape=jax.ShapeDtype...]
where the time goes in v3:
time: 77 us; the launch traced here: 76.9 us
  Pallas kernels  74.4 us (97%)
  local copies, waits for them, and re-layouts  2.42 us (3%)
    pallas_call x1, Pallas kernels, body(): pl.pallas_call(functools.partial(kernel, count), out_shape=jax.ShapeDtype...  74.4 us
    unnamed x1, local copies, waits for them, and re-layouts  2.42 us

profile of v3, /device:TPU:1, one launch (start us, length us, event | category | flops | bytes accessed | tf_op | source)
XLA Modules:
  0.0 76.9 jit_solution(17669171184915950)
XLA Ops:
  0.0 74.4 %shard_map.55 = f32[2048,128]{1,0:T(8,128)} custom-call(f32[32,3,16,256]{3,2,1,0:T(8,128)} %bitcast.13, f32[16,16]{1,0:T(8,128)} %mach.1, bf16[8,2,64,64]{3,2,1,0:T(8,128)(2,1)} %bitcast.15, s32[8]{0:T(128)} %offs.1, f32[2048,128]{1,0:T(8,128)} %bitcast.14), custom_call_target="tpu_custom_call" | custom-call | tf_op jit(solution)/shard_map/pallas_call | solution.py:553
  74.4 2.4 %copy.9 = f32[16,16,4,256]{3,2,1,0:T(4,128)} copy(f32[16,16,4,256]{3,2,1,0:T(4,128)} %bitcast.12) | data formatting | bytes 2097152

commit v4 on v3

--- a/solution.py
+++ b/solution.py
@@ -28,7 +28,7 @@
 
 def kernel(count, les, mach, tiles, offs, state, out, *refs):
     (v0, v1, *zv), refs = refs[:4], refs[4:]
-    f, zf, xh, yh, refs = *(refs[k * STAGES:(k + 1) * STAGES] for k in range(4)), refs[4 * STAGES:]
+    f, zf, xh, yh, sb, refs = *(refs[k * STAGES:(k + 1) * STAGES] for k in range(4)), refs[4 * STAGES:4 * STAGES + 2], refs[4 * STAGES + 2:]
     s, tb, (stage, lb, wk, mb, tl, mc, send, recv, local) = refs[:2], refs[2:4], refs[4:]
     ix, iy, ig = lax.axis_index("gx"), lax.axis_index("gy"), lax.axis_index("grp")
     has_l, has_r = ix > 0, ix < count - 1
@@ -158,6 +158,8 @@
 
     def rims(n, h):
         half = slice(None) if h is None else h
+        if n % 3 == 1:
+            return Sides(((sb[n // 3].at[0, :, :, half], xh[n].at[0, :, :, half]), (sb[n // 3].at[1, :, :, half], xh[n].at[1, :, :, half])))
         return Sides(((f[n].at[pl.ds(EX + NA - EX, EX), :, half, ROWS, :], xh[n].at[0, :, :, half]),
                       (f[n].at[pl.ds(EX, EX), :, half, ROWS, :], xh[n].at[1, :, :, half])))
 
@@ -441,8 +443,6 @@
     def mend(k):
         n = 3 * k + 1
         for h in range(2):
-            sides[n][h].drain()
-            sent.remove(sides[n][h])
             terms[k][h].wait()
 
             def go(i):
@@ -505,6 +505,11 @@
             if n % 3 == 1:
                 mend_halo(n // 3, h)
             correct(n, h)
+            if n % 3 == 0:
+                for j in range(EX):
+                    for c in range(4):
+                        sb[n // 3][0, j, c, h] = f[n + 1][EX + NA - EX + j, c, h, ROWS, :]
+                        sb[n // 3][1, j, c, h] = f[n + 1][EX + j, c, h, ROWS, :]
             if n + 1 < STAGES:
                 pl.when(sooner)(sides[n + 1][h].start)
         if n % 3 == 0:
@@ -564,6 +569,7 @@
                 *[pltpu.VMEM((NA, 4, NY, L), F32)] * STAGES,
                 *[pltpu.VMEM((2, EX, 4, 2, NY, L), F32)] * STAGES,
                 *[pltpu.VMEM((NA, 4, 2, NY, L), F32)] * STAGES,
+                *[pltpu.VMEM((2, EX, 4, 2, NY, L), F32)] * 2,
                 *[pltpu.VMEM((NA, 3, 2, NY, L), F32)] * 2,
                 *[pltpu.VMEM((4, 2, 4, 3, NY, L), F32)] * 2,
                 pltpu.VMEM((NA * NY * 8, L), F32),

time: 77 us -> 72.2 us (0.938)
  Pallas kernels: 74.4 us -> 69 us
    pallas_call x1, Pallas kernels: 74.4 us -> 69 us  [body(): pl.pallas_call(functools.partial(kernel, count), out_shape=jax.ShapeDtype...]
where the time goes in v4:
time: 72.2 us; the launch traced here: 71.5 us
  Pallas kernels  69 us (96%)
  local copies, waits for them, and re-layouts  2.42 us (3%)
    pallas_call x1, Pallas kernels, body(): pl.pallas_call(functools.partial(kernel, count), out_shape=jax.ShapeDtype...  69 us
    unnamed x1, local copies, waits for them, and re-layouts  2.42 us

profile of v4, /device:TPU:1, one launch (start us, length us, event | category | flops | bytes accessed | tf_op | source)
XLA Modules:
  0.0 71.5 jit_solution(10896278879942069312)
XLA Ops:
  0.0 69.0 %shard_map.55 = f32[2048,128]{1,0:T(8,128)} custom-call(f32[32,3,16,256]{3,2,1,0:T(8,128)} %bitcast.13, f32[16,16]{1,0:T(8,128)} %mach.1, bf16[8,2,64,64]{3,2,1,0:T(8,128)(2,1)} %bitcast.15, s32[8]{0:T(128)} %offs.1, f32[2048,128]{1,0:T(8,128)} %bitcast.14), custom_call_target="tpu_custom_call" | custom-call | tf_op jit(solution)/shard_map/pallas_call | solution.py:558
  69.1 2.4 %copy.9 = f32[16,16,4,256]{3,2,1,0:T(4,128)} copy(f32[16,16,4,256]{3,2,1,0:T(4,128)} %bitcast.12) | data formatting | bytes 2097152

commit v5 on v4

--- a/solution.py
+++ b/solution.py
@@ -54,7 +54,7 @@
     loads = []
     for h in range(2):
         loads.append(pltpu.make_async_copy(les.at[:, :, :, pl.ds(L * h, L)], v0.at[pl.ds(1, NX), :, h, ROWS, :], local.at[h]))
-    loads.append(pltpu.make_async_copy(state, stage, local.at[2]))
+    loads.append(pltpu.make_async_copy(state, stage.at[pl.ds(0, NA * NY * 8)], local.at[2]))
     loads.append(pltpu.make_async_copy(tiles, tl, local.at[3]))
     loads.append(pltpu.make_async_copy(mach, mc, local.at[4]))
     for c in loads:
@@ -572,7 +572,7 @@
                 *[pltpu.VMEM((2, EX, 4, 2, NY, L), F32)] * 2,
                 *[pltpu.VMEM((NA, 3, 2, NY, L), F32)] * 2,
                 *[pltpu.VMEM((4, 2, 4, 3, NY, L), F32)] * 2,
-                pltpu.VMEM((NA * NY * 8, L), F32),
+                pltpu.VMEM((NA * NY * 8 + 8, L), F32),
                 pltpu.VMEM((8 * 128, 6 * L), BF16),
                 pltpu.VMEM((6, 768, 64), BF16),
                 pltpu.VMEM((NA, NY, L), F32),

time: 72.2 us -> 72.2 us (level)
  no operation moved by 1% of the time
where the time goes in v5:
time: 72.2 us; the launch traced here: 71.5 us
  Pallas kernels  69 us (96%)
  local copies, waits for them, and re-layouts  2.42 us (3%)
    pallas_call x1, Pallas kernels, body(): pl.pallas_call(functools.partial(kernel, count), out_shape=jax.ShapeDtype...  69 us
    unnamed x1, local copies, waits for them, and re-layouts  2.42 us

profile of v5, /device:TPU:1, one launch (start us, length us, event | category | flops | bytes accessed | tf_op | source)
XLA Modules:
  0.0 71.5 jit_solution(2423277902726864992)
XLA Ops:
  0.0 69.0 %shard_map.55 = f32[2048,128]{1,0:T(8,128)} custom-call(f32[32,3,16,256]{3,2,1,0:T(8,128)} %bitcast.13, f32[16,16]{1,0:T(8,128)} %mach.1, bf16[8,2,64,64]{3,2,1,0:T(8,128)(2,1)} %bitcast.15, s32[8]{0:T(128)} %offs.1, f32[2048,128]{1,0:T(8,128)} %bitcast.14), custom_call_target="tpu_custom_call" | custom-call | tf_op jit(solution)/shard_map/pallas_call | solution.py:558
  69.0 2.4 %copy.9 = f32[16,16,4,256]{3,2,1,0:T(4,128)} copy(f32[16,16,4,256]{3,2,1,0:T(4,128)} %bitcast.12) | data formatting | bytes 2097152

commit v6 on v5

--- a/solution.py
+++ b/solution.py
@@ -492,13 +492,21 @@
             cross[n][1].wait_twin()
             cross[n][2].wait_twin()
             rim(width, lambda x: both(step)(x))
-        for c in cross[n]:
+        cross[n][0].wait_side()
+        if n % 3 == 2:
+            over(EX, NA - EX, functools.partial(correct_rows, n))
+            if n + 1 == STAGES:
+                inner = pltpu.make_async_copy(stage.at[pl.ds(3 * 128, 10 * 128)], out.at[pl.ds(3 * 128, 10 * 128)], local.at[0])
+                inner.start()
+            else:
+                cross[n + 1][0].start()
+        for c in cross[n][1:]:
             c.wait_side()
-        over(0, NA, functools.partial(correct_rows, n))
-        if n + 1 == STAGES:
-            inner = pltpu.make_async_copy(stage.at[pl.ds(3 * 128, 10 * 128)], out.at[pl.ds(3 * 128, 10 * 128)], local.at[0])
-            inner.start()
-        elif n % 3:
+        if n % 3 == 2:
+            rim(EX, functools.partial(correct_rows, n))
+        else:
+            over(0, NA, functools.partial(correct_rows, n))
+        if n % 3 == 1:
             cross[n + 1][0].start()
         for h in range(2):
             sides[n][h].wait()

time: 72.2 us -> 71.8 us (level)
  no operation moved by 1% of the time
where the time goes in v6:
time: 71.8 us; the launch traced here: 71 us
  Pallas kernels  68.6 us (96%)
  local copies, waits for them, and re-layouts  2.42 us (3%)
    pallas_call x1, Pallas kernels, body(): pl.pallas_call(functools.partial(kernel, count), out_shape=jax.ShapeDtype...  68.6 us
    unnamed x1, local copies, waits for them, and re-layouts  2.42 us

profile of v6, /device:TPU:1, one launch (start us, length us, event | category | flops | bytes accessed | tf_op | source)
XLA Modules:
  0.0 71.0 jit_solution(12788415911955858774)
XLA Ops:
  0.0 68.6 %shard_map.55 = f32[2048,128]{1,0:T(8,128)} custom-call(f32[32,3,16,256]{3,2,1,0:T(8,128)} %bitcast.13, f32[16,16]{1,0:T(8,128)} %mach.1, bf16[8,2,64,64]{3,2,1,0:T(8,128)(2,1)} %bitcast.15, s32[8]{0:T(128)} %offs.1, f32[2048,128]{1,0:T(8,128)} %bitcast.14), custom_call_target="tpu_custom_call" | custom-call | tf_op jit(solution)/shard_map/pallas_call | solution.py:566
  68.6 2.4 %copy.9 = f32[16,16,4,256]{3,2,1,0:T(4,128)} copy(f32[16,16,4,256]{3,2,1,0:T(4,128)} %bitcast.12) | data formatting | bytes 2097152
